TPU v7x, 32 devices: a whole 2x2x4 slice. The times are simulated.
32 devices in a mesh: group: 4 (over y, core), tile: 8 (over z, x).
Axes of the slice: x: 2, y: 2, z: 4, core: 2. Of those that a mesh axis runs over, the one named last changes fastest.
Arguments:
- features: bfloat16 [65536, 128], P(('group', 'tile')), may hold values from -6 to 6
- kernel_map: int32 [32, 27, 2048], P(('group', 'tile')), may hold values from 0 to 2560, as said below
- send_order: int32 [32, 2048], P(('group', 'tile')), may hold values from 0 to 2047, each once within a row
- counts: int32 [32], P(('group', 'tile')), may hold values from 1 to 2048, 49152 in all
- first_weight: bfloat16 [27, 128, 128], replicated, may hold values from -0.109375 to 0.109375
- second_weight: bfloat16 [27, 128, 128], replicated, may hold values from -0.109375 to 0.109375
- norm_gain: float32 [128], replicated, may hold values from 0.1 to 1.9
- cotangent: bfloat16 [65536, 128], P(('group', 'tile')), may hold values from -6 to 6
Outputs:
- serial_out: bfloat16 [65536, 128], P(('group', 'tile'))
- grad_features: bfloat16 [65536, 128], P(('group', 'tile'))
- first_grad: float32 [27, 128, 128], replicated
- second_grad: float32 [27, 128, 128], replicated
- gain_grad: float32 [128], replicated
Inputs may be any that keep to these rules, and one draw needn't show every extreme that they name: `kernel_map`: entry [d, k, i] is the row of tile d's table read by voxel slot i for offset k: rows 0 to 255 are the previous tile's slots 256 to 511, then the tile's own 2048 slots, then the next tile's first 256 slots, and 2560 means no neighbour. Offset 13 is the voxel itself. Only slots below 256 read the previous tile, only slots 256 to 511 read the next. `send_order`: each row holds every slot once. `counts`: the largest is exactly 2048.
All inputs are finite; a program needn't handle non-finite values. No bound on the sum of `counts` on one device may be relied on, other than what follows from the above.
Results may differ from a plain program's by a relative error of at most 0.0049.
Values may be sent and summed in bfloat16 or wider, within the bound.
No kernel may reach another device: no remote copies, remote signals or barrier semaphores. Data moves between devices by JAX's collectives and lax.ppermute only.
A program may use at most 192 MiB of HBM per device.

v0:
```python
import jax
import jax.numpy as jnp
from jax import lax
from jax.sharding import PartitionSpec as P

F = 256


def shifted(value, axis, steps):
    count = lax.axis_size(axis)
    initial, last = (max(0, -steps), min(count, count - steps))
    return lax.ppermute(value, axis, [(source, source + steps) for source in range(initial, last)])


def extend(field):
    chans = field.shape[1]
    before = shifted(field[F : 2 * F], ("group", "tile"), 1)
    after = shifted(field[:F], ("group", "tile"), -1)
    zero_row = jnp.zeros((1, chans), field.dtype)
    return jnp.concatenate([before, field, after, zero_row], axis=0)


def fold_table(table_grad):
    slots = table_grad.shape[0] - 2 * F - 1
    own = table_grad[F : F + slots]
    from_prev = shifted(
        table_grad[slots + F : slots + 2 * F].astype(jnp.bfloat16), ("group", "tile"), 1
    ).astype(jnp.float32)
    from_next = shifted(table_grad[:F].astype(jnp.bfloat16), ("group", "tile"), -1).astype(
        jnp.float32
    )
    own = own.at[:F].add(from_prev)
    own = own.at[F : 2 * F].add(from_next)
    return own


def gather_rows(table, neighbours):
    slots = neighbours.shape[1]
    offsets = neighbours.shape[0]
    rows = jnp.take(table, neighbours.T, axis=0)
    return rows.reshape(slots, offsets * table.shape[1])


def convolve(table, neighbours, weights):
    offsets, chans_in, chans = weights.shape
    gathered = gather_rows(table, neighbours)
    return jnp.dot(
        gathered, weights.reshape(offsets * chans_in, chans), preferred_element_type=jnp.float32
    )


def convolve_back(table, neighbours, weights, grad_out):
    offsets, chans_in, chans = weights.shape
    slots = neighbours.shape[1]
    gathered = gather_rows(table, neighbours)
    weight_term = lax.dot_general(
        gathered, grad_out, (((0,), (0,)), ((), ())), preferred_element_type=jnp.float32
    )
    terms = lax.dot_general(
        grad_out,
        weights.reshape(offsets * chans_in, chans),
        (((1,), (1,)), ((), ())),
        preferred_element_type=jnp.float32,
    )
    terms = terms.reshape(slots * offsets, chans_in)
    table_grad = jax.ops.segment_sum(terms, neighbours.T.reshape(-1), num_segments=table.shape[0])
    return (weight_term.reshape(offsets, chans_in, chans), table_grad)


def norm_act(first, gain, live):
    centre = jnp.mean(first, axis=-1, keepdims=True)
    centred = first - centre
    variance = jnp.mean(centred * centred, axis=-1, keepdims=True)
    inv_std = lax.rsqrt(variance + 1e-05)
    unit = centred * inv_std
    normed = unit * gain
    hidden = (jax.nn.gelu(normed) * live).astype(jnp.bfloat16)
    return (hidden, unit, inv_std, normed)


def norm_back(grad_hidden, normed, unit, inv_std, gain, live):
    _, pull = jax.vjp(jax.nn.gelu, normed)
    grad_normed = pull(grad_hidden * live)[0]
    gain_term = jnp.sum(grad_normed * unit, axis=0)
    grad_unit = grad_normed * gain
    centred_grad = (
        grad_unit
        - jnp.mean(grad_unit, axis=-1, keepdims=True)
        - unit * jnp.mean(grad_unit * unit, axis=-1, keepdims=True)
    )
    return ((inv_std * centred_grad).astype(jnp.bfloat16), gain_term)


def to_serial(rows):
    return lax.all_to_all(rows, ("group", "tile"), split_axis=0, concat_axis=0, tiled=True)


def to_spatial(rows):
    return lax.all_to_all(rows, ("group", "tile"), split_axis=0, concat_axis=0, tiled=True)


def local(
    features, kernel_map, send_order, counts, first_weight, second_weight, norm_gain, cotangent
):
    slots, chans = features.shape
    neighbours = kernel_map[0]
    order = send_order[0]
    live = (jnp.arange(slots, dtype=jnp.int32) < counts[0]).astype(jnp.float32)[:, None]
    masked = (features.astype(jnp.float32) * live).astype(jnp.bfloat16)
    table_x = extend(masked)
    first = convolve(table_x, neighbours, first_weight)
    hidden, unit, inv_std, normed = norm_act(first, norm_gain, live)
    table_h = extend(hidden)
    second = convolve(table_h, neighbours, second_weight)
    block = ((masked.astype(jnp.float32) + second) * live).astype(jnp.bfloat16)
    ordered = jnp.take(block, order, axis=0)
    serial_out = to_serial(ordered)
    slotted = to_spatial(cotangent)
    grad_block = jnp.zeros_like(slotted).at[order].set(slotted)
    grad_live = (grad_block.astype(jnp.float32) * live).astype(jnp.bfloat16)
    second_term, table_grad_h = convolve_back(table_h, neighbours, second_weight, grad_live)
    grad_hidden = fold_table(table_grad_h)
    grad_first, gain_term = norm_back(grad_hidden, normed, unit, inv_std, norm_gain, live)
    first_term, table_grad_x = convolve_back(table_x, neighbours, first_weight, grad_first)
    grad_x = fold_table(table_grad_x) + grad_live.astype(jnp.float32)
    grad_features = (grad_x * live).astype(jnp.bfloat16)
    first_grad, second_grad, gain_grad = lax.psum(
        (first_term, second_term, gain_term), ("group", "tile")
    )
    return (serial_out, grad_features, first_grad, second_grad, gain_grad)


def solution(mesh):
    placed = (
        P(("group", "tile"), None),
        P(("group", "tile"), None, None),
        P(("group", "tile"), None),
        P(("group", "tile")),
        P(),
        P(),
        P(),
        P(("group", "tile"), None),
    )
    return jax.shard_map(
        local,
        mesh=mesh,
        in_specs=placed,
        out_specs=(P(("group", "tile"), None), P(("group", "tile"), None), P(), P(), P()),
        check_vma=False,
    )
```

profile of v0, /device:TPU:0, one launch (start us, length us, event | category | flops | bytes accessed | tf_op | source)
XLA Modules:
  0.0 1435.0 jit_solution(7541587480908522428)
XLA Ops:
  7.2 7.4 all-to-all-start.1
  33.7 192.0 %gather_fusion.1 = bf16[55296,128]{1,0:T(8,128)(2,1)} fusion(bf16[2561,128]{1,0:T(8,128)(2,1)S(1)} %maximum_maximum_fusion, s32[55296]{0:T(1024)S(1)} %broadcast_clamp_fusion), kind=kCustom, calls=%fused_computation.clone | custom fusion | bytes 28532736 | tf_op jit(solution)/shard_map/jit(_take)/gather | solution.py:40
  225.7 22.4 %reshape.269 = bf16[2048,27,128]{2,1,0:T(8,128)(2,1)} reshape(bf16[55296,128]{1,0:T(8,128)(2,1)} %gather_fusion.1) | data formatting | bytes 28311552 | tf_op jit(solution)/shard_map/jit(_take)/gather | solution.py:40
  248.1 13.4 broadcast_select_fusion
  261.5 23.6 %copy.22 = bf16[2048,27,128]{0,2,1:T(8,128)(2,1)} copy(bf16[2048,27,128]{2,1,0:T(8,128)(2,1)} %broadcast_select_fusion) | data formatting | bytes 28311552 | tf_op jit(solution)/shard_map/jit(_take)/select_n | solution.py:40
  285.1 7.3 fusion.32
  294.1 6.4 scatter_custom_fusion
  300.5 11.4 fusion.26
  311.9 28.8 %reshape.248 = f32[55296,128]{1,0:T(8,128)} reshape(f32[2048,3456]{1,0:T(8,128)} %fusion.26) | data formatting | bytes 56623104 | tf_op jit(solution)/shard_map/reshape | solution.py:65
  340.7 293.6 %scatter_custom_fusion.1 = f32[2561,128]{1,0:T(8,128)S(1)} fusion(s32[55296]{0:T(1024)} %reshape.254, f32[55296,128]{1,0:T(8,128)} %reshape.248, f32[]{:T(128)} %constant.138.clone.1), kind=kCustom, calls=%fused_computation.40 | custom fusion | flops 7077888 | bytes 1311744 | tf_op jit(solution)/shard_map/scatter-add | solution.py:66
  656.3 10.7 fusion.2
  667.0 11.7 fusion.33
  678.8 28.8 %reshape.256 = f32[55296,128]{1,0:T(8,128)} reshape(f32[2048,3456]{1,0:T(8,128)} %fusion.33) | data formatting | bytes 56623104 | tf_op jit(solution)/shard_map/reshape | solution.py:65
  707.6 293.6 %scatter_custom_fusion.2 = f32[2561,128]{1,0:T(8,128)S(1)} fusion(s32[55296]{0:T(1024)} %reshape.254, f32[55296,128]{1,0:T(8,128)} %reshape.256, f32[]{:T(128)} %constant.138.clone.1), kind=kCustom, calls=%fused_computation.38 | custom fusion | flops 7077888 | bytes 1311744 | tf_op jit(solution)/shard_map/scatter-add | solution.py:66
  1008.1 192.0 %gather_fusion.2 = bf16[55296,128]{1,0:T(8,128)(2,1)} fusion(bf16[2561,128]{1,0:T(8,128)(2,1)S(1)} %maximum_maximum_fusion.1, s32[55296]{0:T(1024)S(1)} %broadcast_clamp_fusion), kind=kCustom, calls=%fused_computation.1.clone | custom fusion | bytes 28532736 | tf_op jit(solution)/shard_map/jit(_take)/gather | solution.py:40
  1200.1 22.4 %reshape.273 = bf16[2048,27,128]{2,1,0:T(8,128)(2,1)} reshape(bf16[55296,128]{1,0:T(8,128)(2,1)} %gather_fusion.2) | data formatting | bytes 28311552 | tf_op jit(solution)/shard_map/jit(_take)/gather | solution.py:40
  1222.5 13.4 broadcast_select_fusion.1
  1235.9 23.5 %copy.23 = bf16[2048,27,128]{0,2,1:T(8,128)(2,1)} copy(bf16[2048,27,128]{2,1,0:T(8,128)(2,1)} %broadcast_select_fusion.1) | data formatting | bytes 28311552 | tf_op jit(solution)/shard_map/jit(_take)/select_n | solution.py:40
  1259.5 8.5 fusion
  1268.0 9.5 fusion.6
  1277.5 8.1 gather_fusion
  1287.7 10.6 all-to-all-start
  1300.7 42.7 %psum.23 = f32[128]{0:T(128)} all-reduce(f32[128]{0:T(128)S(1)} %get-tuple-element.54), channel_id=1, replica_groups=mesh['group'=4,'tile'=8] {'group','tile'}, use_global_device_ids=true, to_apply=%region_10.12 | all-reduce | flops 128 | bytes 1024 | tf_op jit(solution)/shard_map/psum | solution.py:127
  1348.1 73.5 %all-reduce.3.cloned.1.call-done = (f32[27,128,128]{2,1,0:T(8,128)}, f32[27,128,128]{2,1,0:T(8,128)}) async-done(((f32[27,128,128]{2,1,0:T(8,128)}, f32[27,128,128]{2,1,0:T(8,128)}), (f32[27,128,128]{2,1,0:T(8,128)}, f32[27,128,128]{2,1,0:T(8,128)})) %all-reduce.3.cloned.1.call-update) | async-done | bytes 3538960 | tf_op jit(solution)/shard_map/psum | solution.py:127
  (83 shorter events, 64.5 us)
Async XLA Ops:
  7.2 277.9 %copy-start = (bf16[27,128,128]{2,1,0:T(8,128)(2,1)S(1)}, bf16[27,128,128]{2,1,0:T(8,128)(2,1)}, u32[]{:S(2)}) copy-start(bf16[27,128,128]{2,1,0:T(8,128)(2,1)} %param.22) | copy-start | bytes 2654212
  7.2 286.9 %all-to-all-start.1 = ((bf16[32,64,128]{2,1,0:T(8,128)(2,1)}), bf16[32,64,128]{2,1,0:T(8,128)(2,1)}, u32[]{:S(2)}, u32[]{:S(2)}) async-start(bf16[32,64,128]{2,1,0:T(8,128)(2,1)} %bitcast.61), calls=%async_computation.1 | async-start | bytes 1048576 | tf_op jit(solution)/shard_map/all_to_all | solution.py:99
  14.6 1407.0 %all-reduce.3.cloned.1.call-start = ((), (), s32[]{:S(2)}) async-start(), calls=%async_computation.2 | async-start | bytes 7077888 | tf_op jit(solution)/shard_map/psum | solution.py:127
  17.4 15.9 %collective-permute-start = (bf16[256,128]{1,0:T(8,128)(2,1)}, bf16[256,128]{1,0:T(8,128)(2,1)S(1)}, u32[]{:S(2)}, u32[]{:S(2)}) collective-permute-start(bf16[256,128]{1,0:T(8,128)(2,1)} %get-tuple-element.67), channel_id=1, source_target_pairs={{0,1},{1,2},{2,3},{3,4},{4,5},{5,6},{6,7},{7,8},{8,9},{9,10},{10,1... | collective-permute-start | bytes 196616 | tf_op jit(solution)/shard_map/ppermute | solution.py:12
  21.0 12.3 collective-permute-start.1
  225.7 22.5 %copy-start.6 = (pred[2048,27]{1,0:T(8,128)(4,1)S(1)}, pred[2048,27]{1,0:T(8,128)(4,1)}, u32[]{:S(2)}) copy-start(pred[2048,27]{1,0:T(8,128)(4,1)} %copy.15) | copy-start | bytes 165892
  285.1 15.4 %copy-start.7 = (bf16[27,128,128]{2,1,0:T(8,128)(2,1)S(1)}, bf16[27,128,128]{2,1,0:T(8,128)(2,1)}, u32[]{:S(2)}) copy-start(bf16[27,128,128]{2,1,0:T(8,128)(2,1)} %param.23) | copy-start | bytes 2654212
  292.4 1.0 copy-start.2
  300.5 959.0 %copy-start.4 = (bf16[2048,128]{1,0:T(8,128)(2,1)}, bf16[2048,128]{1,0:T(8,128)(2,1)S(1)}, u32[]{:S(2)}) copy-start(bf16[2048,128]{1,0:T(8,128)(2,1)S(1)} %scatter_custom_fusion) | copy-start | bytes 1572868
  311.9 334.7 %copy-start.10 = (f32[128]{0:T(128)S(1)}, f32[128]{0:T(128)}, u32[]{:S(2)}) copy-start(f32[128]{0:T(128)} %param.24) | copy-start | bytes 1540
  634.4 6.8 collective-permute-start.4
  639.1 7.5 collective-permute-start.5
  649.5 0.8 copy-start.5
  649.5 17.5 %copy-start.3 = (f32[2048,128]{1,0:T(8,128)S(1)}, f32[2048,128]{1,0:T(8,128)}, u32[]{:S(2)}) copy-start(f32[2048,128]{1,0:T(8,128)} %copy-done.2) | copy-start | bytes 3145732
  650.9 355.7 %collective-permute-start.2 = (bf16[256,128]{1,0:T(8,128)(2,1)}, bf16[256,128]{1,0:T(8,128)(2,1)S(1)}, u32[]{:S(2)}, u32[]{:S(2)}) collective-permute-start(bf16[256,128]{1,0:T(8,128)(2,1)} %get-tuple-element.65), channel_id=1, source_target_pairs={{0,1},{1,2},{2,3},{3,4},{4,5},{5,6},{6,7},{7,8},{8,9},{9,10},{10,1... | collective-permute-start | bytes 196616 | tf_op jit(solution)/shard_map/ppermute | solution.py:12
  654.7 351.9 %collective-permute-start.3 = (bf16[256,128]{1,0:T(8,128)(2,1)}, bf16[256,128]{1,0:T(8,128)(2,1)S(1)}, u32[]{:S(2)}, u32[]{:S(2)}) collective-permute-start(bf16[256,128]{1,0:T(8,128)(2,1)} %get-tuple-element.66), channel_id=1, source_target_pairs={{1,0},{2,1},{3,2},{4,3},{5,4},{6,5},{7,6},{8,7},{9,8},{10,9},{11,1... | collective-permute-start | bytes 196616 | tf_op jit(solution)/shard_map/ppermute | solution.py:12
  1001.9 341.5 %collective-permute-start.6 = (bf16[256,128]{1,0:T(8,128)(2,1)}, bf16[256,128]{1,0:T(8,128)(2,1)S(1)}, u32[]{:S(2)}, u32[]{:S(2)}) collective-permute-start(bf16[256,128]{1,0:T(8,128)(2,1)} %get-tuple-element.62), channel_id=1, source_target_pairs={{0,1},{1,2},{2,3},{3,4},{4,5},{5,6},{6,7},{7,8},{8,9},{9,10},{10,1... | collective-permute-start | bytes 196616 | tf_op jit(solution)/shard_map/ppermute | solution.py:12
  1267.9 9.5 copy-start.8
  1267.9 17.6 %copy-start.9 = (pred[32,64]{1,0:T(8,128)(4,1)S(1)}, pred[32,64]{1,0:T(8,128)(4,1)}, u32[]{:S(2)}) copy-start(pred[32,64]{1,0:T(8,128)(4,1)} %compare_and_fusion.1) | copy-start | bytes 6148
  1268.0 160.2 %copy-start.1 = (bf16[27,128,128]{2,1,0:T(8,128)(2,1)S(1)}, bf16[27,128,128]{2,1,0:T(8,128)(2,1)}, u32[]{:S(2)}) copy-start(bf16[27,128,128]{2,1,0:T(8,128)(2,1)} %param.22) | copy-start | bytes 2654212
  1287.7 60.4 %all-to-all-start = ((bf16[32,64,128]{2,1,0:T(8,128)(2,1)}), bf16[32,64,128]{2,1,0:T(8,128)(2,1)S(1)}, u32[]{:S(2)}, u32[]{:S(2)}) async-start(bf16[32,64,128]{2,1,0:T(8,128)(2,1)} %broadcast_select_fusion.2), calls=%async_computation | async-start | bytes 1048576 | tf_op jit(solution)/shard_map/all_to_all | solution.py:95
  1299.4 44.7 %collective-permute-start.7 = (bf16[256,128]{1,0:T(8,128)(2,1)S(1)}, bf16[256,128]{1,0:T(8,128)(2,1)S(1)}, u32[]{:S(2)}, u32[]{:S(2)}) collective-permute-start(bf16[256,128]{1,0:T(8,128)(2,1)S(1)} %get-tuple-element.61), channel_id=1, source_target_pairs={{1,0},{2,1},{3,2},{4,3},{5,4},{6,5},{7,6},{8,7},{9,8},{10,9},{11,1... | collective-permute-start | bytes 196616 | tf_op jit(solution)/shard_map/ppermute | solution.py:12
Sparse Core Ops, SparseCore 0:
  1268.1 153.4 all-reduce.2
where the time goes:
time: 1440 us; the launch traced here: 1430 us
  other arithmetic  633 us (44%)
  local copies, waits for them, and re-layouts  565 us (39%)
  waiting for transfers between devices  79.7 us (6%)
  matrix products  59.2 us (4%)
  blocking collectives  42.7 us (3%)
  starting transfers between devices  40.2 us (3%)
  between operations  15.1 us (1%)
    scatter-add x2, other arithmetic, convolve_back(): jax.ops.segment_sum(terms, neighbours.T.reshape(-1), num_segments=table.s...  587 us
    gather x4, local copies, waits for them, and re-layouts, gather_rows(): rows = jnp.take(table, neighbours.T, axis=0)  429 us
    psum x1, waiting for transfers between devices, local(): lax.psum((first_term, second_term, gain_term), ('group', 'tile'))  73.5 us
    reshape x2, local copies, waits for them, and re-layouts, convolve_back(): terms = terms.reshape(slots * offsets, chans_in)  57.6 us
    select_n x3, local copies, waits for them, and re-layouts, gather_rows(): rows = jnp.take(table, neighbours.T, axis=0)  47.5 us
    psum x1, blocking collectives, local(): lax.psum((first_term, second_term, gain_term), ('group', 'tile'))  42.7 us
  transfers between devices with their start and end apart: 11, of which 3 were waited for; matrix products, arithmetic and copies ran while one was open for 63% of the time, Pallas kernels for 0%

commit v1 on v0

v1 whole, which is shorter than its diff:
```python
import jax
import jax.numpy as jnp
from jax import lax
from jax.experimental import pallas as pl
from jax.experimental.pallas import tpu as pltpu
from jax.sharding import PartitionSpec as P

F = 256
B = 256
SHIFT = 8
NT = (((1,), (1,)), ((), ()))
TN = (((0,), (0,)), ((), ()))


def shifted(value, axis, steps):
    count = lax.axis_size(axis)
    initial, last = (max(0, -steps), min(count, count - steps))
    return lax.ppermute(value, axis, [(source, source + steps) for source in range(initial, last)])


def faces_of(field):
    before = shifted(field[F : 2 * F], ("group", "tile"), 1)
    after = shifted(field[:F], ("group", "tile"), -1)
    return before, after


def lane_replicated(row):
    parts = [
        jnp.broadcast_to(row[:, j : j + 128], (128, 128)).T for j in range(0, row.shape[1], 128)
    ]
    return jnp.concatenate(parts, axis=0)


def onehot_rows(index, width):
    lanes = lax.broadcasted_iota(jnp.int32, index.shape, 1)
    parts = [
        jnp.where(index == lanes + j, 1.0, 0.0).astype(jnp.bfloat16) for j in range(0, width, 128)
    ]
    return jnp.concatenate(parts, axis=1)


def onehot_cols(row, height):
    shape = (height, row.shape[1])
    return jnp.where(
        jnp.broadcast_to(row, shape) == lax.broadcasted_iota(jnp.int32, shape, 0), 1.0, 0.0
    ).astype(jnp.bfloat16)


def side_mask(entry, side, slots):
    if side == 0:
        return entry < F
    return (entry >= slots + F) & (entry < slots + 2 * F)


def gather_body(map_ref, field_ref, before_ref, after_ref, weight_ref, *refs, keep):
    if keep:
        rows_ref, out_ref, table_ref = refs
    else:
        out_ref, table_ref = refs
    slots, chans = field_ref.shape
    groups = slots // B
    k = pl.program_id(0)

    @pl.when(k == 0)
    def _():
        out_ref[...] = jnp.zeros_like(out_ref)
        for a in range(groups):
            table_ref[:, a * chans : (a + 1) * chans] = field_ref[a * B : (a + 1) * B, :]

    for block in range(slots // F):
        at = slice(block * F, (block + 1) * F)
        entry = lane_replicated(map_ref[pl.ds(k, 1), at])
        own = entry - F
        low, high = own & (B - 1), own >> SHIFT
        picked = jnp.dot(
            onehot_rows(low, B), table_ref[...], preferred_element_type=jnp.float32
        )
        rows = jnp.where(high == 0, picked[:, :chans], 0.0)
        for a in range(1, groups):
            rows = jnp.where(high == a, picked[:, a * chans : (a + 1) * chans], rows)
        if block < 2:
            face = (before_ref, after_ref)[block][...]
            crossing = jnp.dot(
                onehot_rows(entry & (F - 1), F), face, preferred_element_type=jnp.float32
            )
            rows = jnp.where(side_mask(entry, block, slots), crossing, rows)
        rows = rows.astype(jnp.bfloat16)
        if keep:
            rows_ref[0, at, :] = rows
        out_ref[at, :] += jnp.dot(rows, weight_ref[0], preferred_element_type=jnp.float32)


def resident(shape):
    return pl.BlockSpec(shape, lambda k: (0,) * len(shape))


def per_offset(shape):
    return pl.BlockSpec((1,) + shape, lambda k: (k,) + (0,) * len(shape))


PARAMS = pltpu.CompilerParams(
    dimension_semantics=("arbitrary",), vmem_limit_bytes=56 * 1024 * 1024
)


def gather_convolve(neighbours, field, before, after, weights, keep):
    offsets, slots = neighbours.shape
    chans = field.shape[1]
    out_specs = [resident((slots, chans))]
    out_shape = [jax.ShapeDtypeStruct((slots, chans), jnp.float32)]
    if keep:
        out_specs = [per_offset((slots, chans))] + out_specs
        out_shape = [jax.ShapeDtypeStruct((offsets, slots, chans), jnp.bfloat16)] + out_shape
    return pl.pallas_call(
        lambda *refs: gather_body(*refs, keep=keep),
        grid=(offsets,),
        in_specs=[
            resident((offsets, slots)),
            resident((slots, chans)),
            resident((F, chans)),
            resident((F, chans)),
            per_offset((chans, chans)),
        ],
        out_specs=out_specs,
        out_shape=out_shape,
        scratch_shapes=[pltpu.VMEM((B, slots // B * chans), jnp.bfloat16)],
        compiler_params=PARAMS,
        name="gather_convolve",
    )(neighbours, field, before, after, weights)


def scatter_body(map_ref, grad_ref, weight_ref, *refs, keep):
    if keep:
        sums_ref, out_ref = refs
    else:
        (out_ref,) = refs
    slots, chans = grad_ref.shape
    groups = slots // B
    k = pl.program_id(0)

    @pl.when(k == 0)
    def _():
        out_ref[...] = jnp.zeros_like(out_ref)

    def finish(at, sums):
        sums = sums.astype(jnp.bfloat16)
        if keep:
            sums_ref[0, at, :] = sums
        out_ref[at, :] += lax.dot_general(
            sums, weight_ref[0], NT, preferred_element_type=jnp.float32
        )

    total = None
    for block in range(slots // F):
        at = slice(block * F, (block + 1) * F)
        row = map_ref[pl.ds(k, 1), at]
        entry = lane_replicated(row)
        high = (entry - F) >> SHIFT
        grad = grad_ref[at, :].astype(jnp.float32)
        spread = jnp.concatenate(
            [jnp.where(high == a, grad, 0.0).astype(jnp.bfloat16) for a in range(groups)], axis=1
        )
        term = jnp.dot(
            onehot_cols((row - F) & (B - 1), B), spread, preferred_element_type=jnp.float32
        )
        total = term if total is None else total + term
        if block < 2:
            crossing = jnp.where(side_mask(entry, block, slots), grad, 0.0).astype(jnp.bfloat16)
            start = 0 if block == 0 else slots + F
            finish(
                slice(start, start + F),
                jnp.dot(
                    onehot_cols(row & (F - 1), F), crossing, preferred_element_type=jnp.float32
                ),
            )
    for a in range(groups):
        finish(slice(F + a * B, F + (a + 1) * B), total[:, a * chans : (a + 1) * chans])


def scatter_convolve(neighbours, grad, weights, keep):
    offsets, slots = neighbours.shape
    chans = grad.shape[1]
    rows = slots + 2 * F
    out_specs = [resident((rows, chans))]
    out_shape = [jax.ShapeDtypeStruct((rows, chans), jnp.float32)]
    if keep:
        out_specs = [per_offset((rows, chans))] + out_specs
        out_shape = [jax.ShapeDtypeStruct((offsets, rows, chans), jnp.bfloat16)] + out_shape
    return pl.pallas_call(
        lambda *refs: scatter_body(*refs, keep=keep),
        grid=(offsets,),
        in_specs=[
            resident((offsets, slots)),
            resident((slots, chans)),
            per_offset((chans, chans)),
        ],
        out_specs=out_specs,
        out_shape=out_shape,
        compiler_params=PARAMS,
        name="scatter_convolve",
    )(neighbours, grad, weights)


def weight_body(rows_ref, sums_ref, grad_ref, table_ref, first_ref, second_ref):
    first_ref[0] = lax.dot_general(
        rows_ref[0], grad_ref[...], TN, preferred_element_type=jnp.float32
    )
    second_ref[0] = lax.dot_general(
        table_ref[...], sums_ref[0], TN, preferred_element_type=jnp.float32
    )


def weight_grads(rows, sums, grad, table):
    offsets, slots, chans = rows.shape
    shape = jax.ShapeDtypeStruct((offsets, chans, chans), jnp.float32)
    return pl.pallas_call(
        weight_body,
        grid=(offsets,),
        in_specs=[
            per_offset((slots, chans)),
            per_offset(sums.shape[1:]),
            resident((slots, chans)),
            resident(table.shape),
        ],
        out_specs=[per_offset((chans, chans)), per_offset((chans, chans))],
        out_shape=[shape, shape],
        compiler_params=PARAMS,
        name="weight_grads",
    )(rows, sums, grad, table)


def fold_table(table_grad):
    slots = table_grad.shape[0] - 2 * F
    own = table_grad[F : F + slots]
    from_prev = shifted(
        table_grad[slots + F :].astype(jnp.bfloat16), ("group", "tile"), 1
    ).astype(jnp.float32)
    from_next = shifted(table_grad[:F].astype(jnp.bfloat16), ("group", "tile"), -1).astype(
        jnp.float32
    )
    own = own.at[:F].add(from_prev)
    own = own.at[F : 2 * F].add(from_next)
    return own


def norm_act(first, gain, live):
    centre = jnp.mean(first, axis=-1, keepdims=True)
    centred = first - centre
    variance = jnp.mean(centred * centred, axis=-1, keepdims=True)
    inv_std = lax.rsqrt(variance + 1e-05)
    unit = centred * inv_std
    normed = unit * gain
    hidden = (jax.nn.gelu(normed) * live).astype(jnp.bfloat16)
    return (hidden, unit, inv_std, normed)


def norm_back(grad_hidden, normed, unit, inv_std, gain, live):
    _, pull = jax.vjp(jax.nn.gelu, normed)
    grad_normed = pull(grad_hidden * live)[0]
    gain_term = jnp.sum(grad_normed * unit, axis=0)
    grad_unit = grad_normed * gain
    centred_grad = (
        grad_unit
        - jnp.mean(grad_unit, axis=-1, keepdims=True)
        - unit * jnp.mean(grad_unit * unit, axis=-1, keepdims=True)
    )
    return ((inv_std * centred_grad).astype(jnp.bfloat16), gain_term)


def to_serial(rows):
    return lax.all_to_all(rows, ("group", "tile"), split_axis=0, concat_axis=0, tiled=True)


def to_spatial(rows):
    return lax.all_to_all(rows, ("group", "tile"), split_axis=0, concat_axis=0, tiled=True)


def local(
    features, kernel_map, send_order, counts, first_weight, second_weight, norm_gain, cotangent
):
    slots, chans = features.shape
    neighbours = kernel_map[0]
    order = send_order[0]
    live = (jnp.arange(slots, dtype=jnp.int32) < counts[0]).astype(jnp.float32)[:, None]
    masked = (features.astype(jnp.float32) * live).astype(jnp.bfloat16)
    before_x, after_x = faces_of(masked)
    slotted = to_spatial(cotangent)
    rows_x, first = gather_convolve(neighbours, masked, before_x, after_x, first_weight, True)
    hidden, unit, inv_std, normed = norm_act(first, norm_gain, live)
    before_h, after_h = faces_of(hidden)
    grad_block = jnp.zeros_like(slotted).at[order].set(slotted)
    grad_live = (grad_block.astype(jnp.float32) * live).astype(jnp.bfloat16)
    sums, table_grad_h = scatter_convolve(neighbours, grad_live, second_weight, True)
    grad_hidden = fold_table(table_grad_h)
    grad_first, gain_term = norm_back(grad_hidden, normed, unit, inv_std, norm_gain, live)
    table_h = jnp.concatenate([before_h, hidden, after_h], axis=0)
    first_term, second_term = weight_grads(rows_x, sums, grad_first, table_h)
    first_grad, second_grad, gain_grad = lax.psum(
        (first_term, second_term, gain_term), ("group", "tile")
    )
    (second,) = gather_convolve(neighbours, hidden, before_h, after_h, second_weight, False)
    block = ((masked.astype(jnp.float32) + second) * live).astype(jnp.bfloat16)
    ordered = jnp.take(block, order, axis=0)
    serial_out = to_serial(ordered)
    (table_grad_x,) = scatter_convolve(neighbours, grad_first, first_weight, False)
    grad_x = fold_table(table_grad_x) + grad_live.astype(jnp.float32)
    grad_features = (grad_x * live).astype(jnp.bfloat16)
    return (serial_out, grad_features, first_grad, second_grad, gain_grad)


def solution(mesh):
    placed = (
        P(("group", "tile"), None),
        P(("group", "tile"), None, None),
        P(("group", "tile"), None),
        P(("group", "tile")),
        P(),
        P(),
        P(),
        P(("group", "tile"), None),
    )
    return jax.shard_map(
        local,
        mesh=mesh,
        in_specs=placed,
        out_specs=(P(("group", "tile"), None), P(("group", "tile"), None), P(), P(), P()),
        check_vma=False,
    )
```

time: 1440 us -> 438 us (0.30)
  other arithmetic: 633 us -> 17.6 us
  local copies, waits for them, and re-layouts: 565 us -> 23 us
  Pallas kernels: 0 us -> 268 us
  matrix products: 59.2 us -> 0 us
  waiting for transfers between devices: 79.7 us -> 26.9 us
    scatter-add x2 -> x0, other arithmetic: 587 us -> none  [convolve_back(): jax.ops.segment_sum(terms, neighbours.T.reshape(-1), num_segments=table.s...]
    gather x4 -> x0, local copies, waits for them, and re-layouts: 429 us -> none  [gather_rows(): rows = jnp.take(table, neighbours.T, axis=0)]
    pallas_call x0 -> x5, Pallas kernels: none -> 268 us  [the longest x2 137 us: gather_convolve(): pl.pallas_call(lambda *refs: gather_body(*refs, keep=keep), grid=(offsets...]
    dot_general x6 -> x0, matrix products: 59.2 us -> none  [the longest x2 23.2 us: convolve_back(): lax.dot_general(grad_out, weights.reshape(offsets * chans_in, chans), (((...]
    psum x1, waiting for transfers between devices: 73.5 us -> 14.8 us  [local(): lax.psum((first_term, second_term, gain_term), ('group', 'tile'))]
    reshape x2 -> x0, local copies, waits for them, and re-layouts: 57.6 us -> none  [convolve_back(): terms = terms.reshape(slots * offsets, chans_in)]
    select_n x3 -> x0, local copies, waits for them, and re-layouts: 47.5 us -> none  [gather_rows(): rows = jnp.take(table, neighbours.T, axis=0)]
    select_n x3 -> x0, other arithmetic: 27.8 us -> none  [gather_rows(): rows = jnp.take(table, neighbours.T, axis=0)]
  transfers between devices with their start and end apart: 11 -> 11, of which waited for: 3 -> 2; matrix products, arithmetic and copies ran while one was open for 63% -> 5% of each run, Pallas kernels for 0% -> 49%
where the time goes in v1:
time: 438 us; the launch traced here: 437 us
  Pallas kernels  268 us (61%)
  starting transfers between devices  45.1 us (10%)
  blocking collectives  40.9 us (9%)
  waiting for transfers between devices  26.9 us (6%)
  local copies, waits for them, and re-layouts  23 us (5%)
  other arithmetic  17.6 us (4%)
  between operations  15.1 us (3%)
    pallas_call x2, Pallas kernels, gather_convolve(): pl.pallas_call(lambda *refs: gather_body(*refs, keep=keep), grid=(offsets...  137 us
    pallas_call x2, Pallas kernels, scatter_convolve(): pl.pallas_call(lambda *refs: scatter_body(*refs, keep=keep), grid=(offset...  105 us
    psum x1, blocking collectives, local(): lax.psum((first_term, second_term, gain_term), ('group', 'tile'))  40.9 us
    pallas_call x1, Pallas kernels, weight_grads(): pl.pallas_call(weight_body, grid=(offsets,), in_specs=[per_offset((slots,...  27 us
    ppermute x8, starting transfers between devices, shifted(): lax.ppermute(value, axis, [(source, source + steps) for source in range(i...  22.8 us
    all_to_all x1, starting transfers between devices, to_serial(): lax.all_to_all(rows, ('group', 'tile'), split_axis=0, concat_axis=0, tile...  14.9 us
    psum x1, waiting for transfers between devices, local(): lax.psum((first_term, second_term, gain_term), ('group', 'tile'))  14.8 us
    all_to_all x1, waiting for transfers between devices, to_spatial(): lax.all_to_all(rows, ('group', 'tile'), split_axis=0, concat_axis=0, tile...  12.1 us
  transfers between devices with their start and end apart: 11, of which 2 were waited for; matrix products, arithmetic and copies ran while one was open for 5% of the time, Pallas kernels for 49%

profile of v1, /device:TPU:0, one launch (start us, length us, event | category | flops | bytes accessed | tf_op | source)
XLA Modules:
  0.0 437.0 jit_solution(4800092833081864722)
XLA Ops:
  7.2 7.3 %all-to-all-start.1 = ((bf16[32,64,128]{2,1,0:T(8,128)(2,1)}), bf16[32,64,128]{2,1,0:T(8,128)(2,1)S(1)}, u32[]{:S(2)}, u32[]{:S(2)}) async-start(bf16[32,64,128]{2,1,0:T(8,128)(2,1)} %bitcast.18), calls=%async_computation.1 | async-start | bytes 1048576 | tf_op jit(solution)/shard_map/all_to_all | solution.py:275
  14.5 1.7 copy.15
  18.8 12.1 %all-to-all-done.1 = bf16[32,64,128]{2,1,0:T(8,128)(2,1)S(1)} async-done(((bf16[32,64,128]{2,1,0:T(8,128)(2,1)}), bf16[32,64,128]{2,1,0:T(8,128)(2,1)S(1)}, u32[]{:S(2)}, u32[]{:S(2)}) %all-to-all-start.1) | async-done | bytes 524320 | tf_op jit(solution)/shard_map/all_to_all | solution.py:275
  30.9 5.9 %scatter_custom_fusion = bf16[2048,128]{1,0:T(8,128)(2,1)S(1)} fusion(s32[2048]{0:T(1024)S(1)} %bitcast.21, bf16[2048,128]{1,0:T(8,128)(2,1)S(1)} %bitcast.19, bf16[]{:T(256)} %constant.133.clone.1), kind=kCustom, calls=%fused_computation.24 | custom fusion | bytes 524290 | tf_op jit(solution)/shard_map/scatter | solution.py:291
  37.9 2.8 collective-permute-start
  42.0 52.4 %scatter_convolve.2 = (bf16[27,2560,128]{2,1,0:T(8,128)(2,1)}, f32[2560,128]{1,0:T(8,128)}) custom-call(s32[27,2048]{1,0:T(8,128)} %bitcast.12, bf16[2048,128]{1,0:T(8,128)(2,1)} %get-tuple-element.82.refs_1_, bf16[27,128,128]{2,1,0:T(8,128)(2,1)} %refs_2_.2), custom_call_target="tpu_custom_call" | custom-call | tf_op jit(solution)/shard_map/scatter_convolve/pallas_call | solution.py:189
  94.4 1.5 convert.8
  96.6 4.5 %collective-permute-start.4 = (bf16[256,128]{1,0:T(8,128)(2,1)}, bf16[256,128]{1,0:T(8,128)(2,1)S(1)}, u32[]{:S(2)}, u32[]{:S(2)}) collective-permute-start(bf16[256,128]{1,0:T(8,128)(2,1)} %get-tuple-element.75), channel_id=1, source_target_pairs={{0,1},{1,2},{2,3},{3,4},{4,5},{5,6},{6,7},{7,8},{8,9},{9,10},{10,1... | collective-permute-start | bytes 196616 | tf_op jit(solution)/shard_map/ppermute | solution.py:18
  103.7 68.3 %gather_convolve.2 = (bf16[27,2048,128]{2,1,0:T(8,128)(2,1)}, f32[2048,128]{1,0:T(8,128)}) custom-call(s32[27,2048]{1,0:T(8,128)} %bitcast.13, bf16[2048,128]{1,0:T(8,128)(2,1)} %copy-done.6, bf16[256,128]{1,0:T(8,128)(2,1)} %copy-done.12, bf16[256,128]{1,0:T(8,128)(2,1)} %copy-done.13, bf16[27,128,128]{2,1,0:T(8,128)(2,1)} %refs_2_.3), custom_call_target="tpu_custom_call" | custom-call | tf_op jit(solution)/shard_map/gather_convolve/pallas_call | solution.py:114
  172.0 2.3 reduce_sum.45
  175.7 1.8 multiply_reduce_fusion
  177.6 2.4 multiply_convert_fusion.1.refs_1_.grad_ref
  180.0 52.3 %scatter_convolve.3 = f32[2560,128]{1,0:T(8,128)} custom-call(s32[27,2048]{1,0:T(8,128)} %bitcast.14, bf16[2048,128]{1,0:T(8,128)(2,1)} %multiply_convert_fusion.1.refs_1_.grad_ref, bf16[27,128,128]{2,1,0:T(8,128)(2,1)} %refs_2_.3), custom_call_target="tpu_custom_call" | custom-call | tf_op jit(solution)/shard_map/scatter_convolve/pallas_call | solution.py:189
  233.7 4.7 %collective-permute-start.2 = (bf16[256,128]{1,0:T(8,128)(2,1)S(1)}, bf16[256,128]{1,0:T(8,128)(2,1)S(1)}, u32[]{:S(2)}, u32[]{:S(2)}) collective-permute-start(bf16[256,128]{1,0:T(8,128)(2,1)S(1)} %get-tuple-element.77), channel_id=1, source_target_pairs={{0,1},{1,2},{2,3},{3,4},{4,5},{5,6},{6,7},{7,8},{8,9},{9,10},{10,1... | collective-permute-start | bytes 196616 | tf_op jit(solution)/shard_map/ppermute | solution.py:18
  239.8 5.4 %collective-permute-start.6 = (bf16[256,128]{1,0:T(8,128)(2,1)S(1)}, bf16[256,128]{1,0:T(8,128)(2,1)S(1)}, u32[]{:S(2)}, u32[]{:S(2)}) collective-permute-start(bf16[256,128]{1,0:T(8,128)(2,1)S(1)} %get-tuple-element.73), channel_id=1, source_target_pairs={{0,1},{1,2},{2,3},{3,4},{4,5},{5,6},{6,7},{7,8},{8,9},{9,10},{10,1... | collective-permute-start | bytes 196616 | tf_op jit(solution)/shard_map/ppermute | solution.py:18
  245.2 1.5 collective-permute-start.7
  247.6 27.0 %weight_grads.1 = (f32[27,128,128]{2,1,0:T(8,128)}, f32[27,128,128]{2,1,0:T(8,128)}) custom-call(bf16[27,2048,128]{2,1,0:T(8,128)(2,1)} %get-tuple-element.61.rows_ref, bf16[27,2560,128]{2,1,0:T(8,128)(2,1)} %get-tuple-element.62.sums_ref, bf16[2048,128]{1,0:T(8,128)(2,1)} %multiply_convert_fusion.1.refs_1_.grad_ref, bf16[2560,128]{1,0:T(8,128)(2,1)} %pad_maximum_fusion.table_ref), custom_call_target="tpu_custom_call" | custom-call | tf_op jit(solution)/shard_map/weight_grads/pallas_call | solution.py:216
  276.4 68.3 %gather_convolve.3 = f32[2048,128]{1,0:T(8,128)} custom-call(s32[27,2048]{1,0:T(8,128)} %bitcast.15, bf16[2048,128]{1,0:T(8,128)(2,1)} %copy-done.2, bf16[256,128]{1,0:T(8,128)(2,1)} %copy-done.10, bf16[256,128]{1,0:T(8,128)(2,1)} %copy-done.11, bf16[27,128,128]{2,1,0:T(8,128)(2,1)} %refs_2_.2), custom_call_target="tpu_custom_call" | custom-call | tf_op jit(solution)/shard_map/gather_convolve/pallas_call | solution.py:114
  344.7 2.4 multiply_convert_fusion
  347.2 6.2 %gather_fusion = bf16[2048,128]{1,0:T(8,128)(2,1)S(1)} fusion(bf16[2048,128]{1,0:T(8,128)(2,1)S(1)} %get-tuple-element.81, s32[2048]{0:T(1024)S(1)} %broadcast_clamp_fusion), kind=kCustom, calls=%fused_computation | custom fusion | bytes 1056768 | tf_op jit(solution)/shard_map/jit(_take)/gather | solution.py:303
  354.5 14.9 %all-to-all-start = ((bf16[32,64,128]{2,1,0:T(8,128)(2,1)}), bf16[32,64,128]{2,1,0:T(8,128)(2,1)S(1)}, u32[]{:S(2)}, u32[]{:S(2)}) async-start(bf16[32,64,128]{2,1,0:T(8,128)(2,1)} %broadcast_select_fusion), calls=%async_computation | async-start | bytes 1048576 | tf_op jit(solution)/shard_map/all_to_all | solution.py:271
  369.4 40.9 %psum.23 = f32[128]{0:T(128)} all-reduce(f32[128]{0:T(128)S(1)} %get-tuple-element.65), channel_id=1, replica_groups=mesh['group'=4,'tile'=8] {'group','tile'}, use_global_device_ids=true, to_apply=%region_8.0 | all-reduce | flops 128 | bytes 1024 | tf_op jit(solution)/shard_map/psum | solution.py:298
  410.3 14.8 %all-reduce.3.cloned.1.call-done = (f32[27,128,128]{2,1,0:T(8,128)}, f32[27,128,128]{2,1,0:T(8,128)}) async-done(((f32[27,128,128]{2,1,0:T(8,128)}, f32[27,128,128]{2,1,0:T(8,128)}), (f32[27,128,128]{2,1,0:T(8,128)}, f32[27,128,128]{2,1,0:T(8,128)})) %all-reduce.3.cloned.1.call-update) | async-done | bytes 3538960 | tf_op jit(solution)/shard_map/psum | solution.py:298
  426.0 3.0 copy.25
  (76 shorter events, 17.5 us)
Async XLA Ops:
  7.2 10.3 %copy-start.14 = (s32[1,2048]{1,0:T(1,128)S(1)}, s32[1,2048]{1,0:T(1,128)}, u32[]{:S(2)}) copy-start(s32[1,2048]{1,0:T(1,128)} %param.18) | copy-start | bytes 24580
  7.2 29.5 %copy-start.7 = (bf16[2048,128]{1,0:T(8,128)(2,1)S(1)}, bf16[2048,128]{1,0:T(8,128)(2,1)}, u32[]{:S(2)}) copy-start(bf16[2048,128]{1,0:T(8,128)(2,1)} %param.16) | copy-start | bytes 1572868
  7.2 23.7 %all-to-all-start.1 = ((bf16[32,64,128]{2,1,0:T(8,128)(2,1)}), bf16[32,64,128]{2,1,0:T(8,128)(2,1)S(1)}, u32[]{:S(2)}, u32[]{:S(2)}) async-start(bf16[32,64,128]{2,1,0:T(8,128)(2,1)} %bitcast.18), calls=%async_computation.1 | async-start | bytes 1048576 | tf_op jit(solution)/shard_map/all_to_all | solution.py:275
  14.5 410.7 %all-reduce.3.cloned.1.call-start = ((), (), s32[]{:S(2)}) async-start(), calls=%async_computation.2 | async-start | bytes 7077888 | tf_op jit(solution)/shard_map/psum | solution.py:298
  36.7 57.7 %copy-start.4 = (bf16[2048,128]{1,0:T(8,128)(2,1)}, bf16[2048,128]{1,0:T(8,128)(2,1)S(1)}, u32[]{:S(2)}) copy-start(bf16[2048,128]{1,0:T(8,128)(2,1)S(1)} %scatter_custom_fusion) | copy-start | bytes 1572868
  37.9 58.0 %copy-start.6 = (bf16[2048,128]{1,0:T(8,128)(2,1)}, bf16[2048,128]{1,0:T(8,128)(2,1)S(1)}, u32[]{:S(2)}) copy-start(bf16[2048,128]{1,0:T(8,128)(2,1)S(1)} %get-tuple-element.83.refs_1_) | copy-start | bytes 1572868
  37.9 64.6 %collective-permute-start = (bf16[256,128]{1,0:T(8,128)(2,1)S(1)}, bf16[256,128]{1,0:T(8,128)(2,1)S(1)}, u32[]{:S(2)}, u32[]{:S(2)}) collective-permute-start(bf16[256,128]{1,0:T(8,128)(2,1)S(1)} %get-tuple-element.79), channel_id=1, source_target_pairs={{0,1},{1,2},{2,3},{3,4},{4,5},{5,6},{6,7},{7,8},{8,9},{9,10},{10,1... | collective-permute-start | bytes 196616 | tf_op jit(solution)/shard_map/ppermute | solution.py:18
  40.7 61.8 %collective-permute-start.1 = (bf16[256,128]{1,0:T(8,128)(2,1)S(1)}, bf16[256,128]{1,0:T(8,128)(2,1)S(1)}, u32[]{:S(2)}, u32[]{:S(2)}) collective-permute-start(bf16[256,128]{1,0:T(8,128)(2,1)S(1)} %get-tuple-element.78), channel_id=1, source_target_pairs={{1,0},{2,1},{3,2},{4,3},{5,4},{6,5},{7,6},{8,7},{9,8},{10,9},{11,1... | collective-permute-start | bytes 196616 | tf_op jit(solution)/shard_map/ppermute | solution.py:18
  94.4 2.2 copy-start.3
  96.6 79.0 %collective-permute-start.4 = (bf16[256,128]{1,0:T(8,128)(2,1)}, bf16[256,128]{1,0:T(8,128)(2,1)S(1)}, u32[]{:S(2)}, u32[]{:S(2)}) collective-permute-start(bf16[256,128]{1,0:T(8,128)(2,1)} %get-tuple-element.75), channel_id=1, source_target_pairs={{0,1},{1,2},{2,3},{3,4},{4,5},{5,6},{6,7},{7,8},{8,9},{9,10},{10,1... | collective-permute-start | bytes 196616 | tf_op jit(solution)/shard_map/ppermute | solution.py:18
  101.2 74.5 %collective-permute-start.5 = (bf16[256,128]{1,0:T(8,128)(2,1)}, bf16[256,128]{1,0:T(8,128)(2,1)S(1)}, u32[]{:S(2)}, u32[]{:S(2)}) collective-permute-start(bf16[256,128]{1,0:T(8,128)(2,1)} %get-tuple-element.74), channel_id=1, source_target_pairs={{1,0},{2,1},{3,2},{4,3},{5,4},{6,5},{7,6},{8,7},{9,8},{10,9},{11,1... | collective-permute-start | bytes 196616 | tf_op jit(solution)/shard_map/ppermute | solution.py:18
  172.0 3.0 copy-start
  177.6 69.2 %copy-start.2 = (bf16[2048,128]{1,0:T(8,128)(2,1)}, bf16[2048,128]{1,0:T(8,128)(2,1)S(1)}, u32[]{:S(2)}) copy-start(bf16[2048,128]{1,0:T(8,128)(2,1)S(1)} %get-tuple-element.71.refs_1_) | copy-start | bytes 1572868
  233.7 13.0 %collective-permute-start.2 = (bf16[256,128]{1,0:T(8,128)(2,1)S(1)}, bf16[256,128]{1,0:T(8,128)(2,1)S(1)}, u32[]{:S(2)}, u32[]{:S(2)}) collective-permute-start(bf16[256,128]{1,0:T(8,128)(2,1)S(1)} %get-tuple-element.77), channel_id=1, source_target_pairs={{0,1},{1,2},{2,3},{3,4},{4,5},{5,6},{6,7},{7,8},{8,9},{9,10},{10,1... | collective-permute-start | bytes 196616 | tf_op jit(solution)/shard_map/ppermute | solution.py:18
  238.4 8.3 %collective-permute-start.3 = (bf16[256,128]{1,0:T(8,128)(2,1)S(1)}, bf16[256,128]{1,0:T(8,128)(2,1)S(1)}, u32[]{:S(2)}, u32[]{:S(2)}) collective-permute-start(bf16[256,128]{1,0:T(8,128)(2,1)S(1)} %get-tuple-element.76), channel_id=1, source_target_pairs={{1,0},{2,1},{3,2},{4,3},{5,4},{6,5},{7,6},{8,7},{9,8},{10,9},{11,1... | collective-permute-start | bytes 196616 | tf_op jit(solution)/shard_map/ppermute | solution.py:18
  239.8 34.9 %collective-permute-start.6 = (bf16[256,128]{1,0:T(8,128)(2,1)S(1)}, bf16[256,128]{1,0:T(8,128)(2,1)S(1)}, u32[]{:S(2)}, u32[]{:S(2)}) collective-permute-start(bf16[256,128]{1,0:T(8,128)(2,1)S(1)} %get-tuple-element.73), channel_id=1, source_target_pairs={{0,1},{1,2},{2,3},{3,4},{4,5},{5,6},{6,7},{7,8},{8,9},{9,10},{10,1... | collective-permute-start | bytes 196616 | tf_op jit(solution)/shard_map/ppermute | solution.py:18
  245.2 99.5 %collective-permute-start.7 = (bf16[256,128]{1,0:T(8,128)(2,1)S(1)}, bf16[256,128]{1,0:T(8,128)(2,1)S(1)}, u32[]{:S(2)}, u32[]{:S(2)}) collective-permute-start(bf16[256,128]{1,0:T(8,128)(2,1)S(1)} %get-tuple-element.72), channel_id=1, source_target_pairs={{1,0},{2,1},{3,2},{4,3},{5,4},{6,5},{7,6},{8,7},{9,8},{10,9},{11,1... | collective-permute-start | bytes 196616 | tf_op jit(solution)/shard_map/ppermute | solution.py:18
  246.7 27.9 %copy-start.10 = (bf16[256,128]{1,0:T(8,128)(2,1)}, bf16[256,128]{1,0:T(8,128)(2,1)S(1)}, u32[]{:S(2)}) copy-start(bf16[256,128]{1,0:T(8,128)(2,1)S(1)} %collective-permute-done.2.refs_2_) | copy-start | bytes 196612
  246.7 27.9 %copy-start.11 = (bf16[256,128]{1,0:T(8,128)(2,1)}, bf16[256,128]{1,0:T(8,128)(2,1)S(1)}, u32[]{:S(2)}) copy-start(bf16[256,128]{1,0:T(8,128)(2,1)S(1)} %collective-permute-done.3.refs_3_) | copy-start | bytes 196612
  276.3 68.4 %copy-start.5 = (bf16[2048,128]{1,0:T(8,128)(2,1)S(1)}, bf16[2048,128]{1,0:T(8,128)(2,1)}, u32[]{:S(2)}) copy-start(bf16[2048,128]{1,0:T(8,128)(2,1)} %copy-done.4) | copy-start | bytes 1572868
  276.3 68.4 %copy-start.8 = (bf16[2048,128]{1,0:T(8,128)(2,1)S(1)}, bf16[2048,128]{1,0:T(8,128)(2,1)}, u32[]{:S(2)}) copy-start(bf16[2048,128]{1,0:T(8,128)(2,1)} %param.16) | copy-start | bytes 1572868
  347.2 6.2 %copy-start.15 = (pred[32,64]{1,0:T(8,128)(4,1)S(1)}, pred[32,64]{1,0:T(8,128)(4,1)}, u32[]{:S(2)}) copy-start(pred[32,64]{1,0:T(8,128)(4,1)} %compare_and_fusion) | copy-start | bytes 6148
  354.5 55.8 %all-to-all-start = ((bf16[32,64,128]{2,1,0:T(8,128)(2,1)}), bf16[32,64,128]{2,1,0:T(8,128)(2,1)S(1)}, u32[]{:S(2)}, u32[]{:S(2)}) async-start(bf16[32,64,128]{2,1,0:T(8,128)(2,1)} %broadcast_select_fusion), calls=%async_computation | async-start | bytes 1048576 | tf_op jit(solution)/shard_map/all_to_all | solution.py:271
  425.9 3.0 copy-start.9
  (5 other events, 5.7 us)
Sparse Core Ops, SparseCore 0:
  274.8 150.3 all-reduce.2

commit v2 on v0

v2 whole, which is shorter than its diff:
```python
import jax
import jax.numpy as jnp
from jax import lax
from jax.experimental import pallas as pl
from jax.experimental.pallas import tpu as pltpu
from jax.sharding import PartitionSpec as P

F = 256
B = 256
SHIFT = 8
WIDE = 1024
EPS = 1e-05
GELU_SCALE = 0.7978845608028654
GELU_CUBIC = 0.044715
AXES = ("group", "tile")
NT = (((1,), (1,)), ((), ()))
PARAMS = pltpu.CompilerParams(
    dimension_semantics=("arbitrary",), vmem_limit_bytes=58 * 1024 * 1024
)


def shifted(value, steps):
    count = lax.axis_size(AXES)
    initial, last = (max(0, -steps), min(count, count - steps))
    return lax.ppermute(value, AXES, [(source, source + steps) for source in range(initial, last)])


def mm(a, b):
    return jnp.dot(a, b, preferred_element_type=jnp.float32)


def lane_replicated(row):
    parts = [
        jnp.broadcast_to(row[:, j : j + 128], (128, 128)).T for j in range(0, row.shape[1], 128)
    ]
    return jnp.concatenate(parts, axis=0)


def onehot_rows(index, width):
    lanes = lax.broadcasted_iota(jnp.int32, index.shape, 1)
    parts = [
        jnp.where(index == lanes + j, 1.0, 0.0).astype(jnp.bfloat16) for j in range(0, width, 128)
    ]
    return jnp.concatenate(parts, axis=1)


def onehot_cols(row, height):
    shape = (height, row.shape[1])
    return jnp.where(
        jnp.broadcast_to(row, shape) == lax.broadcasted_iota(jnp.int32, shape, 0), 1.0, 0.0
    ).astype(jnp.bfloat16)


def side_mask(entry, side, slots):
    if side == 0:
        return entry < F
    return (entry >= slots + F) & (entry < slots + 2 * F)


def alive(start, size, count, chans):
    rows = lax.broadcasted_iota(jnp.int32, (size, chans), 0) + start
    return jnp.where(rows < count, 1.0, 0.0)


def load_table(table_ref, field, start, size, chans):
    for a in range(start // B, (start + size) // B):
        at = a * B - start
        table_ref[:, a * chans : (a + 1) * chans] = field[at : at + B]


def pick(index, table_ref, chans):
    picked = mm(onehot_rows(index & (B - 1), B), table_ref[...])
    high = index >> SHIFT
    rows = jnp.where(high == 0, picked[:, :chans], 0.0)
    for a in range(1, table_ref.shape[1] // chans):
        rows = jnp.where(high == a, picked[:, a * chans : (a + 1) * chans], rows)
    return rows


def drop(row, index, value, groups):
    high = index >> SHIFT
    spread = jnp.concatenate(
        [jnp.where(high == a, value, 0.0).astype(jnp.bfloat16) for a in range(groups)], axis=1
    )
    return mm(onehot_cols(row & (B - 1), B), spread)


def normalise(first, gain):
    centred = first - jnp.mean(first, axis=-1, keepdims=True)
    inv_std = lax.rsqrt(jnp.mean(centred * centred, axis=-1, keepdims=True) + EPS)
    unit = centred * inv_std
    normed = unit * gain
    bent = jnp.tanh(GELU_SCALE * (normed + GELU_CUBIC * (normed * normed * normed)))
    return unit, inv_std, normed, bent


def gather_step(map_ref, before_ref, after_ref, weight_ref, out_ref, table_ref, slots, chans):
    step = pl.program_id(0)
    unroll = weight_ref.shape[0]
    weight = weight_ref[...].reshape(unroll * chans, chans)
    for start in range(0, slots, WIDE):
        size = min(WIDE, slots - start)
        found = []
        for u in range(unroll):
            entry = lane_replicated(map_ref[pl.ds(step * unroll + u, 1), start : start + size])
            rows = pick(entry - F, table_ref, chans)
            parts = []
            for side, face_ref in enumerate((before_ref, after_ref)):
                at = side * F - start
                if 0 <= at < size:
                    near = entry[at : at + F]
                    crossing = mm(onehot_rows(near & (F - 1), F), face_ref[...])
                    parts.append(
                        jnp.where(side_mask(near, side, slots), crossing, rows[at : at + F])
                    )
            if parts:
                parts.append(rows[len(parts) * F :])
                rows = jnp.concatenate(parts, axis=0)
            found.append(rows.astype(jnp.bfloat16))
        out_ref[start : start + size, :] += mm(jnp.concatenate(found, axis=1), weight)


def first_layer_body(
    count_ref, map_ref, field_ref, before_ref, after_ref, weight_ref, gain_ref,
    first_ref, hidden_ref, table_ref,
):
    slots, chans = field_ref.shape
    step = pl.program_id(0)

    @pl.when(step == 0)
    def _():
        first_ref[...] = jnp.zeros_like(first_ref)
        for start in range(0, slots, B):
            field = field_ref[start : start + B, :].astype(jnp.float32)
            field = (field * alive(start, B, count_ref[0], chans)).astype(jnp.bfloat16)
            load_table(table_ref, field, start, B, chans)

    gather_step(map_ref, before_ref, after_ref, weight_ref, first_ref, table_ref, slots, chans)

    @pl.when(step == pl.num_programs(0) - 1)
    def _():
        for start in range(0, slots, B):
            at = slice(start, start + B)
            _, _, normed, bent = normalise(first_ref[at, :], gain_ref[...])
            act = 0.5 * normed * (1.0 + bent)
            hidden_ref[at, :] = (act * alive(start, B, count_ref[0], chans)).astype(jnp.bfloat16)


def second_layer_body(
    count_ref, map_ref, order_ref, skip_ref, field_ref, before_ref, after_ref, weight_ref,
    serial_ref, second_ref, table_ref,
):
    slots, chans = field_ref.shape
    step = pl.program_id(0)

    @pl.when(step == 0)
    def _():
        second_ref[...] = jnp.zeros_like(second_ref)
        load_table(table_ref, field_ref, 0, slots, chans)

    gather_step(map_ref, before_ref, after_ref, weight_ref, second_ref, table_ref, slots, chans)

    @pl.when(step == pl.num_programs(0) - 1)
    def _():
        for start in range(0, slots, B):
            at = slice(start, start + B)
            live = alive(start, B, count_ref[0], chans)
            masked = skip_ref[at, :].astype(jnp.float32) * live
            block = ((masked + second_ref[at, :]) * live).astype(jnp.bfloat16)
            load_table(table_ref, block, start, B, chans)
        for start in range(0, slots, WIDE):
            size = min(WIDE, slots - start)
            index = lane_replicated(order_ref[:, start : start + size])
            serial_ref[start : start + size, :] = pick(index, table_ref, chans).astype(
                jnp.bfloat16
            )


def scatter_step(map_ref, weight_ref, grad_ref, turned_ref, total_ref, wgrad_ref):
    slots, chans = grad_ref.shape
    groups = slots // B
    step = pl.program_id(0)
    unroll = weight_ref.shape[0]
    near, own = [], []
    for u in range(unroll):
        row = map_ref[pl.ds(step * unroll + u, 1), :]
        entry = lane_replicated(row)
        grad = grad_ref[...].astype(jnp.float32)
        own.append(drop(row - F, entry - F, grad, groups).astype(jnp.bfloat16))
        faces = []
        for side in range(2):
            at = slice(side * F, (side + 1) * F)
            crossing = jnp.where(side_mask(entry[at], side, slots), grad[at], 0.0)
            faces.append(
                mm(onehot_cols(row[:, at] & (F - 1), F), crossing.astype(jnp.bfloat16)).astype(
                    jnp.bfloat16
                )
            )
        near.append(faces)
    back = jnp.concatenate([weight_ref[u] for u in range(unroll)], axis=1)
    wide = None
    starts = [0] + [F + a * B for a in range(groups)] + [F + slots]
    for n, start in enumerate(starts):
        if 0 < n <= groups:
            a = n - 1
            piece = [own[u][:, a * chans : (a + 1) * chans] for u in range(unroll)]
        else:
            piece = [near[u][0 if n == 0 else 1] for u in range(unroll)]
        piece = jnp.concatenate(piece, axis=1)
        at = slice(start, start + piece.shape[0])
        total_ref[at, :] += lax.dot_general(piece, back, NT, preferred_element_type=jnp.float32)
        term = mm(turned_ref[:, at], piece)
        wide = term if wide is None else wide + term
    for u in range(unroll):
        wgrad_ref[step * unroll + u] = wide[:, u * chans : (u + 1) * chans]


def turn_table(turned_ref, before, own, after):
    slots = own.shape[0]
    turned_ref[:, :F] = before.T
    turned_ref[:, F : F + slots] = own.T
    turned_ref[:, F + slots :] = after.T


def give_back(total_ref, own_ref, prev_ref, next_ref):
    slots = own_ref.shape[0]
    own_ref[...] = total_ref[F : F + slots, :]
    prev_ref[...] = total_ref[:F, :].astype(jnp.bfloat16)
    next_ref[...] = total_ref[F + slots :, :].astype(jnp.bfloat16)


def second_back_body(
    count_ref, map_ref, order_ref, slotted_ref, field_ref, before_ref, after_ref, weight_ref,
    own_ref, prev_ref, next_ref, wgrad_ref, grad_ref, turned_ref, total_ref,
):
    slots, chans = field_ref.shape
    step = pl.program_id(0)

    @pl.when(step == 0)
    def _():
        total_ref[...] = jnp.zeros_like(total_ref)
        turn_table(turned_ref, before_ref[...], field_ref[...], after_ref[...])
        order = order_ref[...]
        placed = drop(
            order, lane_replicated(order), slotted_ref[...].astype(jnp.float32), slots // B
        )
        for a in range(slots // B):
            live = alive(a * B, B, count_ref[0], chans)
            grad_ref[a * B : (a + 1) * B, :] = (
                placed[:, a * chans : (a + 1) * chans] * live
            ).astype(jnp.bfloat16)

    scatter_step(map_ref, weight_ref, grad_ref, turned_ref, total_ref, wgrad_ref)

    @pl.when(step == pl.num_programs(0) - 1)
    def _():
        give_back(total_ref, own_ref, prev_ref, next_ref)


def first_back_body(
    count_ref, map_ref, first_ref, upper_ref, from_prev_ref, from_next_ref, gain_ref,
    field_ref, before_ref, after_ref, weight_ref,
    own_ref, prev_ref, next_ref, wgrad_ref, grad_ref, turned_ref, total_ref,
):
    slots, chans = field_ref.shape
    step = pl.program_id(0)

    @pl.when(step == 0)
    def _():
        total_ref[...] = jnp.zeros_like(total_ref)
        gain_term = jnp.zeros((1, chans), jnp.float32)
        turned_ref[:, :F] = before_ref[...].T
        turned_ref[:, F + slots :] = after_ref[...].T
        for start in range(0, slots, B):
            at = slice(start, start + B)
            live = alive(start, B, count_ref[0], chans)
            masked = (field_ref[at, :].astype(jnp.float32) * live).astype(jnp.bfloat16)
            turned_ref[:, F + start : F + start + B] = masked.T
            upper = upper_ref[at, :]
            if start == 0:
                upper = upper + from_prev_ref[...].astype(jnp.float32)
            if start == F:
                upper = upper + from_next_ref[...].astype(jnp.float32)
            unit, inv_std, normed, bent = normalise(first_ref[at, :], gain_ref[...])
            inner = GELU_SCALE * (1.0 + 3.0 * GELU_CUBIC * (normed * normed))
            slope = 0.5 * (1.0 + bent) + 0.5 * normed * (1.0 - bent * bent) * inner
            grad_normed = slope * (upper * live)
            gain_term = gain_term + jnp.sum(grad_normed * unit, axis=0, keepdims=True)
            grad_unit = grad_normed * gain_ref[...]
            centred = (
                grad_unit
                - jnp.mean(grad_unit, axis=-1, keepdims=True)
                - unit * jnp.mean(grad_unit * unit, axis=-1, keepdims=True)
            )
            grad_ref[at, :] = (inv_std * centred).astype(jnp.bfloat16)
        lanes = lax.broadcasted_iota(jnp.int32, (chans, chans), 0)
        wgrad_ref[wgrad_ref.shape[0] - 1] = jnp.where(
            lanes == 0, jnp.broadcast_to(gain_term, (chans, chans)), 0.0
        )

    scatter_step(map_ref, weight_ref, grad_ref, turned_ref, total_ref, wgrad_ref)

    @pl.when(step == pl.num_programs(0) - 1)
    def _():
        give_back(total_ref, own_ref, prev_ref, next_ref)


def call(body, name, operands, stepped, outputs, scratch):
    offsets = operands[stepped].shape[0]
    unroll = 3 if offsets % 3 == 0 else 1

    def whole(shape):
        return pl.BlockSpec(shape, lambda k: (0,) * len(shape))

    specs = []
    for n, operand in enumerate(operands):
        if n == 0:
            specs.append(pl.BlockSpec(memory_space=pltpu.SMEM))
        elif n == stepped:
            specs.append(pl.BlockSpec((unroll,) + operand.shape[1:], lambda k: (k, 0, 0)))
        else:
            specs.append(whole(operand.shape))
    return pl.pallas_call(
        body,
        grid=(offsets // unroll,),
        in_specs=specs,
        out_specs=[whole(shape) for shape, _ in outputs],
        out_shape=[jax.ShapeDtypeStruct(shape, dtype) for shape, dtype in outputs],
        scratch_shapes=[pltpu.VMEM(shape, dtype) for shape, dtype in scratch],
        compiler_params=PARAMS,
        name=name,
    )(*operands)


def swap_rows(rows):
    return lax.all_to_all(rows, AXES, split_axis=0, concat_axis=0, tiled=True)


def local(
    features, kernel_map, send_order, counts, first_weight, second_weight, norm_gain, cotangent
):
    slots, chans = features.shape
    neighbours = kernel_map[0]
    offsets = neighbours.shape[0]
    gain = norm_gain[None, :]
    bf16, f32 = jnp.bfloat16, jnp.float32
    rows16, rows32 = ((slots, chans), bf16), ((slots, chans), f32)
    face16 = ((F, chans), bf16)
    table16 = ((B, slots // B * chans), bf16)
    turned16 = ((chans, slots + 2 * F), bf16)
    total32 = ((slots + 2 * F, chans), f32)

    ends = jnp.arange(2 * F, dtype=jnp.int32)[:, None] < counts[0]
    ends_x = (features[: 2 * F].astype(f32) * ends.astype(f32)).astype(bf16)
    before_x, after_x = shifted(ends_x[F:], 1), shifted(ends_x[:F], -1)
    slotted = swap_rows(cotangent)
    first, hidden = call(
        first_layer_body, "first_layer",
        (counts, neighbours, features, before_x, after_x, first_weight, gain), 5,
        (rows32, rows16), (table16,),
    )
    before_h, after_h = shifted(hidden[F : 2 * F], 1), shifted(hidden[:F], -1)
    upper, upper_prev, upper_next, second_term, grad_live = call(
        second_back_body, "second_back",
        (counts, neighbours, send_order, slotted, hidden, before_h, after_h, second_weight), 7,
        (rows32, face16, face16, ((offsets, chans, chans), f32), rows16), (turned16, total32),
    )
    second_grad = lax.psum(second_term, AXES)
    from_prev, from_next = shifted(upper_next, 1), shifted(upper_prev, -1)
    lower, lower_prev, lower_next, first_term = call(
        first_back_body, "first_back",
        (counts, neighbours, first, upper, from_prev, from_next, gain, features, before_x,
         after_x, first_weight), 10,
        (rows32, face16, face16, ((offsets + 1, chans, chans), f32)),
        (rows16, turned16, total32),
    )
    reduced = lax.psum(first_term, ("tile", "group"))
    down_prev, down_next = shifted(lower_next, 1), shifted(lower_prev, -1)
    (ordered,) = call(
        second_layer_body, "second_layer",
        (counts, neighbours, send_order, features, hidden, before_h, after_h, second_weight), 7,
        (rows16,), (rows32, table16),
    )
    serial_out = swap_rows(ordered)
    live = (jnp.arange(slots, dtype=jnp.int32) < counts[0]).astype(f32)[:, None]
    grad_x = lower + grad_live.astype(f32)
    grad_x = grad_x.at[:F].add(down_prev.astype(f32))
    grad_x = grad_x.at[F : 2 * F].add(down_next.astype(f32))
    grad_features = (grad_x * live).astype(bf16)
    return (serial_out, grad_features, reduced[:offsets], second_grad, reduced[offsets, 0])


def solution(mesh):
    placed = (
        P(AXES, None),
        P(AXES, None, None),
        P(AXES, None),
        P(AXES),
        P(),
        P(),
        P(),
        P(AXES, None),
    )
    return jax.shard_map(
        local,
        mesh=mesh,
        in_specs=placed,
        out_specs=(P(AXES, None), P(AXES, None), P(), P(), P()),
        check_vma=False,
    )
```

time: 1440 us -> 481 us (0.33)
  other arithmetic: 633 us -> 2.31 us
  local copies, waits for them, and re-layouts: 565 us -> 12.4 us
  Pallas kernels: 0 us -> 188 us
  waiting for transfers between devices: 79.7 us -> 226 us
  matrix products: 59.2 us -> 0 us
  blocking collectives: 42.7 us -> 0 us
    scatter-add x6 -> x2, other arithmetic: 589 us -> 0.04 us  [the longest x1 0.02 us: local(): grad_x = grad_x.at[F:2 * F].add(down_next.astype(f32))]
    gather x5 -> x0, local copies, waits for them, and re-layouts: 437 us -> none  [the longest x4 429 us: gather_rows(): rows = jnp.take(table, neighbours.T, axis=0)]
    pallas_call x0 -> x4, Pallas kernels: none -> 188 us  [call(): pl.pallas_call(body, grid=(offsets // unroll,), in_specs=specs, out_specs...]
    psum x1 -> x2, waiting for transfers between devices: 73.5 us -> 199 us  [the longest x1 133 us: local(): second_grad = lax.psum(second_term, AXES)]
    dot_general x6 -> x0, matrix products: 59.2 us -> none  [the longest x2 23.2 us: convolve_back(): lax.dot_general(grad_out, weights.reshape(offsets * chans_in, chans), (((...]
    reshape x2 -> x0, local copies, waits for them, and re-layouts: 57.6 us -> none  [convolve_back(): terms = terms.reshape(slots * offsets, chans_in)]
    select_n x3 -> x0, local copies, waits for them, and re-layouts: 47.5 us -> none  [gather_rows(): rows = jnp.take(table, neighbours.T, axis=0)]
    psum x1 -> x0, blocking collectives: 42.7 us -> none  [local(): lax.psum((first_term, second_term, gain_term), ('group', 'tile'))]
  transfers between devices with their start and end apart: 11 -> 12, of which waited for: 3 -> 8; matrix products, arithmetic and copies ran while one was open for 63% -> 2% of each run, Pallas kernels for 0% -> 18%
where the time goes in v2:
time: 481 us
  waiting for transfers between devices  226 us (47%)
  Pallas kernels  188 us (39%)
  starting transfers between devices  37.1 us (8%)
  between operations  14.9 us (3%)
  local copies, waits for them, and re-layouts  12.4 us (3%)
    pallas_call x4, Pallas kernels, call(): pl.pallas_call(body, grid=(offsets // unroll,), in_specs=specs, out_specs...  188 us
    psum x1, waiting for transfers between devices, local(): second_grad = lax.psum(second_term, AXES)  133 us
    psum x1, waiting for transfers between devices, local(): reduced = lax.psum(first_term, ('tile', 'group'))  65.6 us
    ppermute x8, starting transfers between devices, shifted(): lax.ppermute(value, AXES, [(source, source + steps) for source in range(i...  21.5 us
    all_to_all x2, starting transfers between devices, swap_rows(): return lax.all_to_all(rows, AXES, split_axis=0, concat_axis=0, tiled=True)  15.5 us
    ppermute x8, waiting for transfers between devices, shifted(): lax.ppermute(value, AXES, [(source, source + steps) for source in range(i...  14.8 us
    all_to_all x2, waiting for transfers between devices, swap_rows(): return lax.all_to_all(rows, AXES, split_axis=0, concat_axis=0, tiled=True)  12.2 us
  transfers between devices with their start and end apart: 12, of which 8 were waited for; matrix products, arithmetic and copies ran while one was open for 2% of the time, Pallas kernels for 18%

profile of v2, /device:TPU:0, one launch (start us, length us, event | category | flops | bytes accessed | tf_op | source)
XLA Modules:
  0.0 480.8 jit_solution(10277796717881735954)
XLA Ops:
  7.2 7.3 %all-to-all-start.1 = ((bf16[32,64,128]{2,1,0:T(8,128)(2,1)}), bf16[32,64,128]{2,1,0:T(8,128)(2,1)S(1)}, u32[]{:S(2)}, u32[]{:S(2)}) async-start(bf16[32,64,128]{2,1,0:T(8,128)(2,1)} %bitcast.20), calls=%async_computation.1 | async-start | bytes 1048576 | tf_op jit(solution)/shard_map/all_to_all | solution.py:336
  16.2 3.7 collective-permute-start
  19.9 1.3 collective-permute-start.1
  21.2 1.7 copy.15
  22.9 3.2 collective-permute-done.1.after_ref
  26.8 43.9 %first_layer.1 = (f32[2048,128]{1,0:T(8,128)}, bf16[2048,128]{1,0:T(8,128)(2,1)}) custom-call(s32[1]{0:T(128)} %copy.21.count_ref, s32[27,2048]{1,0:T(8,128)} %bitcast.13, bf16[2048,128]{1,0:T(8,128)(2,1)} %field_ref.3, bf16[256,128]{1,0:T(8,128)(2,1)} %copy-done.3, bf16[256,128]{1,0:T(8,128)(2,1)} %copy-done.4, bf16[27,128,128]{2,1,0:T(8,128)(2,1)} %weight_ref.7, ...), custom_call_target="tpu_custom_call" | custom-call | tf_op jit(solution)/shard_map/first_layer/pallas_call | solution.py:323
  71.5 5.5 %collective-permute-start.2 = (bf16[256,128]{1,0:T(8,128)(2,1)S(1)}, bf16[256,128]{1,0:T(8,128)(2,1)S(1)}, u32[]{:S(2)}, u32[]{:S(2)}) collective-permute-start(bf16[256,128]{1,0:T(8,128)(2,1)S(1)} %get-tuple-element.52), channel_id=1, source_target_pairs={{0,1},{1,2},{2,3},{3,4},{4,5},{5,6},{6,7},{7,8},{8,9},{9,10},{10,1... | collective-permute-start | bytes 196616 | tf_op jit(solution)/shard_map/ppermute | solution.py:25
  77.0 1.5 collective-permute-start.3
  78.9 5.7 %collective-permute-done.3.after_ref = bf16[256,128]{1,0:T(8,128)(2,1)S(1)} collective-permute-done((bf16[256,128]{1,0:T(8,128)(2,1)S(1)}, bf16[256,128]{1,0:T(8,128)(2,1)S(1)}, u32[]{:S(2)}, u32[]{:S(2)}) %collective-permute-start.3) | collective-permute-done | bytes 65568 | tf_op jit(solution)/shard_map/ppermute | solution.py:25
  85.4 48.9 %second_back.1 = (f32[2048,128]{1,0:T(8,128)}, bf16[256,128]{1,0:T(8,128)(2,1)}, bf16[256,128]{1,0:T(8,128)(2,1)}, f32[27,128,128]{2,1,0:T(8,128)}, bf16[2048,128]{1,0:T(8,128)(2,1)}) custom-call(s32[1]{0:T(128)} %copy.21.count_ref, s32[27,2048]{1,0:T(8,128)} %bitcast.14, s32[1,2048]{1,0:T(1,128)} %order_ref.3, bf16[2048,128]{1,0:T(8,128)(2,1)} %bitcast.17, ...), custom_call_target="tpu_custom_call" | custom-call | tf_op jit(solution)/shard_map/second_back/pallas_call | solution.py:323
  134.3 3.2 collective-permute-start.4
  137.4 1.5 collective-permute-start.5
  139.6 4.8 %collective-permute-done.5.from_next_ref = bf16[256,128]{1,0:T(8,128)(2,1)S(1)} collective-permute-done((bf16[256,128]{1,0:T(8,128)(2,1)}, bf16[256,128]{1,0:T(8,128)(2,1)S(1)}, u32[]{:S(2)}, u32[]{:S(2)}) %collective-permute-start.5) | collective-permute-done | bytes 65568 | tf_op jit(solution)/shard_map/ppermute | solution.py:25
  145.1 50.6 %first_back.1 = (f32[2048,128]{1,0:T(8,128)}, bf16[256,128]{1,0:T(8,128)(2,1)}, bf16[256,128]{1,0:T(8,128)(2,1)}, f32[28,128,128]{2,1,0:T(8,128)}) custom-call(s32[1]{0:T(128)} %copy.21.count_ref, s32[27,2048]{1,0:T(8,128)} %bitcast.15, f32[2048,128]{1,0:T(8,128)} %get-tuple-element.41.first_ref, f32[2048,128]{1,0:T(8,128)} %get-tuple-element.42.upper_ref, ...), custom_call_target="tpu_custom_call" | custom-call | tf_op jit(solution)/shard_map/first_back/pallas_call | solution.py:323
  195.7 44.4 %second_layer.1 = bf16[2048,128]{1,0:T(8,128)(2,1)} custom-call(s32[1]{0:T(128)} %copy.21.count_ref, s32[27,2048]{1,0:T(8,128)} %bitcast.16, s32[1,2048]{1,0:T(1,128)} %order_ref.3, bf16[2048,128]{1,0:T(8,128)(2,1)} %field_ref.3, bf16[2048,128]{1,0:T(8,128)(2,1)} %get-tuple-element.40.field_ref, bf16[256,128]{1,0:T(8,128)(2,1)} %copy-done.5, ...), custom_call_target="tpu_custom_call" | custom-call | tf_op jit(solution)/shard_map/second_layer/pallas_call | solution.py:323
  240.1 8.2 %all-to-all-start = ((bf16[32,64,128]{2,1,0:T(8,128)(2,1)}), bf16[32,64,128]{2,1,0:T(8,128)(2,1)S(1)}, u32[]{:S(2)}, u32[]{:S(2)}) async-start(bf16[32,64,128]{2,1,0:T(8,128)(2,1)} %bitcast.19), calls=%async_computation | async-start | bytes 1048576 | tf_op jit(solution)/shard_map/all_to_all | solution.py:336
  249.1 3.7 collective-permute-start.6
  252.8 1.3 collective-permute-start.7
  254.2 12.2 %all-to-all-done = bf16[32,64,128]{2,1,0:T(8,128)(2,1)S(1)} async-done(((bf16[32,64,128]{2,1,0:T(8,128)(2,1)}), bf16[32,64,128]{2,1,0:T(8,128)(2,1)S(1)}, u32[]{:S(2)}, u32[]{:S(2)}) %all-to-all-start) | async-done | bytes 524320 | tf_op jit(solution)/shard_map/all_to_all | solution.py:336
  267.7 65.6 %all-reduce.3.cloned.1.call-done = f32[28,128,128]{2,1,0:T(8,128)} async-done(((f32[28,128,128]{2,1,0:T(8,128)}), f32[28,128,128]{2,1,0:T(8,128)}) %all-reduce.3.cloned.1.call-update) | async-done | bytes 1835024 | tf_op jit(solution)/shard_map/psum | solution.py:377
  333.2 2.9 slice.72
  336.1 1.2 slice_bitcast_fusion
  337.3 133.0 %all-reduce.5.cloned.1.call-done = f32[27,128,128]{2,1,0:T(8,128)} async-done(((f32[27,128,128]{2,1,0:T(8,128)}), f32[27,128,128]{2,1,0:T(8,128)}) %all-reduce.5.cloned.1.call-update) | async-done | bytes 1769488 | tf_op jit(solution)/shard_map/psum | solution.py:368
  471.1 2.9 copy.23
  (42 shorter events, 8.0 us)
Async XLA Ops:
  7.2 77.4 %all-to-all-start.1 = ((bf16[32,64,128]{2,1,0:T(8,128)(2,1)}), bf16[32,64,128]{2,1,0:T(8,128)(2,1)S(1)}, u32[]{:S(2)}, u32[]{:S(2)}) async-start(bf16[32,64,128]{2,1,0:T(8,128)(2,1)} %bitcast.20), calls=%async_computation.1 | async-start | bytes 1048576 | tf_op jit(solution)/shard_map/all_to_all | solution.py:336
  14.5 318.8 %all-reduce.3.cloned.1.call-start = ((), (), s32[]{:S(2)}) async-start(), calls=%async_computation.2 | async-start | bytes 3670016 | tf_op jit(solution)/shard_map/psum | solution.py:377
  16.2 6.7 %collective-permute-start = (bf16[256,128]{1,0:T(8,128)(2,1)S(1)}, bf16[256,128]{1,0:T(8,128)(2,1)S(1)}, u32[]{:S(2)}, u32[]{:S(2)}) collective-permute-start(bf16[256,128]{1,0:T(8,128)(2,1)S(1)} %get-tuple-element.54), channel_id=1, source_target_pairs={{0,1},{1,2},{2,3},{3,4},{4,5},{5,6},{6,7},{7,8},{8,9},{9,10},{10,1... | collective-permute-start | bytes 196616 | tf_op jit(solution)/shard_map/ppermute | solution.py:25
  19.9 6.2 %collective-permute-start.1 = (bf16[256,128]{1,0:T(8,128)(2,1)S(1)}, bf16[256,128]{1,0:T(8,128)(2,1)S(1)}, u32[]{:S(2)}, u32[]{:S(2)}) collective-permute-start(bf16[256,128]{1,0:T(8,128)(2,1)S(1)} %get-tuple-element.53), channel_id=1, source_target_pairs={{1,0},{2,1},{3,2},{4,3},{5,4},{6,5},{7,6},{8,7},{9,8},{10,9},{11,1... | collective-permute-start | bytes 196616 | tf_op jit(solution)/shard_map/ppermute | solution.py:25
  22.9 3.2 copy-start.3
  26.1 0.6 copy-start.4
  71.5 7.3 %collective-permute-start.2 = (bf16[256,128]{1,0:T(8,128)(2,1)S(1)}, bf16[256,128]{1,0:T(8,128)(2,1)S(1)}, u32[]{:S(2)}, u32[]{:S(2)}) collective-permute-start(bf16[256,128]{1,0:T(8,128)(2,1)S(1)} %get-tuple-element.52), channel_id=1, source_target_pairs={{0,1},{1,2},{2,3},{3,4},{4,5},{5,6},{6,7},{7,8},{8,9},{9,10},{10,1... | collective-permute-start | bytes 196616 | tf_op jit(solution)/shard_map/ppermute | solution.py:25
  77.0 7.6 %collective-permute-start.3 = (bf16[256,128]{1,0:T(8,128)(2,1)S(1)}, bf16[256,128]{1,0:T(8,128)(2,1)S(1)}, u32[]{:S(2)}, u32[]{:S(2)}) collective-permute-start(bf16[256,128]{1,0:T(8,128)(2,1)S(1)} %get-tuple-element.51), channel_id=1, source_target_pairs={{1,0},{2,1},{3,2},{4,3},{5,4},{6,5},{7,6},{8,7},{9,8},{10,9},{11,1... | collective-permute-start | bytes 196616 | tf_op jit(solution)/shard_map/ppermute | solution.py:25
  78.9 5.7 %copy-start.5 = (bf16[256,128]{1,0:T(8,128)(2,1)}, bf16[256,128]{1,0:T(8,128)(2,1)S(1)}, u32[]{:S(2)}) copy-start(bf16[256,128]{1,0:T(8,128)(2,1)S(1)} %collective-permute-done.2.before_ref) | copy-start | bytes 196612
  84.6 0.6 copy-start.6
  84.6 0.8 copy-start
  134.3 5.4 %collective-permute-start.4 = (bf16[256,128]{1,0:T(8,128)(2,1)}, bf16[256,128]{1,0:T(8,128)(2,1)S(1)}, u32[]{:S(2)}, u32[]{:S(2)}) collective-permute-start(bf16[256,128]{1,0:T(8,128)(2,1)} %get-tuple-element.43), channel_id=1, source_target_pairs={{0,1},{1,2},{2,3},{3,4},{4,5},{5,6},{6,7},{7,8},{8,9},{9,10},{10,1... | collective-permute-start | bytes 196616 | tf_op jit(solution)/shard_map/ppermute | solution.py:25
  137.4 7.0 %collective-permute-start.5 = (bf16[256,128]{1,0:T(8,128)(2,1)}, bf16[256,128]{1,0:T(8,128)(2,1)S(1)}, u32[]{:S(2)}, u32[]{:S(2)}) collective-permute-start(bf16[256,128]{1,0:T(8,128)(2,1)} %get-tuple-element.44), channel_id=1, source_target_pairs={{1,0},{2,1},{3,2},{4,3},{5,4},{6,5},{7,6},{8,7},{9,8},{10,9},{11,1... | collective-permute-start | bytes 196616 | tf_op jit(solution)/shard_map/ppermute | solution.py:25
  139.6 4.8 %copy-start.7 = (bf16[256,128]{1,0:T(8,128)(2,1)}, bf16[256,128]{1,0:T(8,128)(2,1)S(1)}, u32[]{:S(2)}) copy-start(bf16[256,128]{1,0:T(8,128)(2,1)S(1)} %collective-permute-done.4.from_prev_ref) | copy-start | bytes 196612
  144.5 0.6 copy-start.8
  240.1 9.0 %copy-start.10 = (bf16[256,128]{1,0:T(8,128)(2,1)S(1)}, bf16[256,128]{1,0:T(8,128)(2,1)}, u32[]{:S(2)}) copy-start(bf16[256,128]{1,0:T(8,128)(2,1)} %get-tuple-element.47) | copy-start | bytes 196612
  240.1 12.7 %copy-start.9 = (bf16[256,128]{1,0:T(8,128)(2,1)S(1)}, bf16[256,128]{1,0:T(8,128)(2,1)}, u32[]{:S(2)}) copy-start(bf16[256,128]{1,0:T(8,128)(2,1)} %get-tuple-element.48) | copy-start | bytes 196612
  240.1 14.0 %copy-start.1 = (f32[2048,128]{1,0:T(8,128)S(1)}, f32[2048,128]{1,0:T(8,128)}, u32[]{:S(2)}) copy-start(f32[2048,128]{1,0:T(8,128)} %get-tuple-element.45) | copy-start | bytes 3145732
  240.1 14.0 %copy-start.2 = (bf16[2048,128]{1,0:T(8,128)(2,1)S(1)}, bf16[2048,128]{1,0:T(8,128)(2,1)}, u32[]{:S(2)}) copy-start(bf16[2048,128]{1,0:T(8,128)(2,1)} %get-tuple-element.46) | copy-start | bytes 1572868
  240.1 26.3 %all-to-all-start = ((bf16[32,64,128]{2,1,0:T(8,128)(2,1)}), bf16[32,64,128]{2,1,0:T(8,128)(2,1)S(1)}, u32[]{:S(2)}, u32[]{:S(2)}) async-start(bf16[32,64,128]{2,1,0:T(8,128)(2,1)} %bitcast.19), calls=%async_computation | async-start | bytes 1048576 | tf_op jit(solution)/shard_map/all_to_all | solution.py:336
  248.4 221.9 %all-reduce.5.cloned.1.call-start = ((), (), s32[]{:S(2)}) async-start(), calls=%async_computation.3 | async-start | bytes 3538944 | tf_op jit(solution)/shard_map/psum | solution.py:368
  249.1 17.3 %collective-permute-start.6 = (bf16[256,128]{1,0:T(8,128)(2,1)S(1)}, bf16[256,128]{1,0:T(8,128)(2,1)S(1)}, u32[]{:S(2)}, u32[]{:S(2)}) collective-permute-start(bf16[256,128]{1,0:T(8,128)(2,1)S(1)} %copy-done.10), channel_id=1, source_target_pairs={{0,1},{1,2},{2,3},{3,4},{4,5},{5,6},{6,7},{7,8},{8,9},{9,10},{10,1... | collective-permute-start | bytes 196616 | tf_op jit(solution)/shard_map/ppermute | solution.py:25
  252.8 13.7 %collective-permute-start.7 = (bf16[256,128]{1,0:T(8,128)(2,1)S(1)}, bf16[256,128]{1,0:T(8,128)(2,1)S(1)}, u32[]{:S(2)}, u32[]{:S(2)}) collective-permute-start(bf16[256,128]{1,0:T(8,128)(2,1)S(1)} %copy-done.9), channel_id=1, source_target_pairs={{1,0},{2,1},{3,2},{4,3},{5,4},{6,5},{7,6},{8,7},{9,8},{10,9},{11,1... | collective-permute-start | bytes 196616 | tf_op jit(solution)/shard_map/ppermute | solution.py:25
Sparse Core Ops, SparseCore 0:
  195.8 137.3 all-reduce.2
  339.2 131.0 all-reduce.4

commit v3 on v2

--- a/solution.py
+++ b/solution.py
@@ -94,7 +94,9 @@
     return unit, inv_std, normed, bent
 
 
-def gather_step(map_ref, before_ref, after_ref, weight_ref, out_ref, table_ref, slots, chans):
+def gather_step(
+    map_ref, before_ref, after_ref, weight_ref, out_ref, table_ref, slots, chans, keep_ref=None
+):
     step = pl.program_id(0)
     unroll = weight_ref.shape[0]
     weight = weight_ref[...].reshape(unroll * chans, chans)
@@ -117,12 +119,14 @@
                 parts.append(rows[len(parts) * F :])
                 rows = jnp.concatenate(parts, axis=0)
             found.append(rows.astype(jnp.bfloat16))
+            if keep_ref is not None:
+                keep_ref[u, start : start + size, :] = found[-1]
         out_ref[start : start + size, :] += mm(jnp.concatenate(found, axis=1), weight)
 
 
 def first_layer_body(
     count_ref, map_ref, field_ref, before_ref, after_ref, weight_ref, gain_ref,
-    first_ref, hidden_ref, table_ref,
+    first_ref, hidden_ref, rows_ref, table_ref,
 ):
     slots, chans = field_ref.shape
     step = pl.program_id(0)
@@ -135,7 +139,9 @@
             field = (field * alive(start, B, count_ref[0], chans)).astype(jnp.bfloat16)
             load_table(table_ref, field, start, B, chans)
 
-    gather_step(map_ref, before_ref, after_ref, weight_ref, first_ref, table_ref, slots, chans)
+    gather_step(
+        map_ref, before_ref, after_ref, weight_ref, first_ref, table_ref, slots, chans, rows_ref
+    )
 
     @pl.when(step == pl.num_programs(0) - 1)
     def _():
@@ -176,7 +182,7 @@
             )
 
 
-def scatter_step(map_ref, weight_ref, grad_ref, turned_ref, total_ref, wgrad_ref):
+def scatter_step(map_ref, weight_ref, grad_ref, total_ref, near_ref=None, turned_ref=None, wgrad_ref=None):
     slots, chans = grad_ref.shape
     groups = slots // B
     step = pl.program_id(0)
@@ -196,12 +202,15 @@
                     jnp.bfloat16
                 )
             )
+            if near_ref is not None:
+                near_ref[u, at, :] = faces[-1]
         near.append(faces)
     back = jnp.concatenate([weight_ref[u] for u in range(unroll)], axis=1)
     wide = None
     starts = [0] + [F + a * B for a in range(groups)] + [F + slots]
     for n, start in enumerate(starts):
-        if 0 < n <= groups:
+        inside = 0 < n <= groups
+        if inside:
             a = n - 1
             piece = [own[u][:, a * chans : (a + 1) * chans] for u in range(unroll)]
         else:
@@ -209,17 +218,12 @@
         piece = jnp.concatenate(piece, axis=1)
         at = slice(start, start + piece.shape[0])
         total_ref[at, :] += lax.dot_general(piece, back, NT, preferred_element_type=jnp.float32)
-        term = mm(turned_ref[:, at], piece)
-        wide = term if wide is None else wide + term
-    for u in range(unroll):
-        wgrad_ref[step * unroll + u] = wide[:, u * chans : (u + 1) * chans]
-
-
-def turn_table(turned_ref, before, own, after):
-    slots = own.shape[0]
-    turned_ref[:, :F] = before.T
-    turned_ref[:, F : F + slots] = own.T
-    turned_ref[:, F + slots :] = after.T
+        if inside and wgrad_ref is not None:
+            term = mm(turned_ref[:, a * B : (a + 1) * B], piece)
+            wide = term if wide is None else wide + term
+    if wgrad_ref is not None:
+        for u in range(unroll):
+            wgrad_ref[u] = wide[:, u * chans : (u + 1) * chans]
 
 
 def give_back(total_ref, own_ref, prev_ref, next_ref):
@@ -230,8 +234,8 @@
 
 
 def second_back_body(
-    count_ref, map_ref, order_ref, slotted_ref, field_ref, before_ref, after_ref, weight_ref,
-    own_ref, prev_ref, next_ref, wgrad_ref, grad_ref, turned_ref, total_ref,
+    count_ref, map_ref, order_ref, slotted_ref, field_ref, weight_ref,
+    own_ref, prev_ref, next_ref, wgrad_ref, near_ref, grad_ref, turned_ref, total_ref,
 ):
     slots, chans = field_ref.shape
     step = pl.program_id(0)
@@ -239,7 +243,7 @@
     @pl.when(step == 0)
     def _():
         total_ref[...] = jnp.zeros_like(total_ref)
-        turn_table(turned_ref, before_ref[...], field_ref[...], after_ref[...])
+        turned_ref[...] = field_ref[...].T
         order = order_ref[...]
         placed = drop(
             order, lane_replicated(order), slotted_ref[...].astype(jnp.float32), slots // B
@@ -250,32 +254,31 @@
                 placed[:, a * chans : (a + 1) * chans] * live
             ).astype(jnp.bfloat16)
 
-    scatter_step(map_ref, weight_ref, grad_ref, turned_ref, total_ref, wgrad_ref)
+    scatter_step(map_ref, weight_ref, grad_ref, total_ref, near_ref, turned_ref, wgrad_ref)
 
     @pl.when(step == pl.num_programs(0) - 1)
     def _():
         give_back(total_ref, own_ref, prev_ref, next_ref)
 
 
-def first_back_body(
-    count_ref, map_ref, first_ref, upper_ref, from_prev_ref, from_next_ref, gain_ref,
-    field_ref, before_ref, after_ref, weight_ref,
-    own_ref, prev_ref, next_ref, wgrad_ref, grad_ref, turned_ref, total_ref,
-):
-    slots, chans = field_ref.shape
-    step = pl.program_id(0)
+def weights_body(
+    count_ref, first_ref, upper_ref, from_prev_ref, from_next_ref, gain_ref,
+    before_ref, after_ref, rows_ref, near_ref, partial_ref,
+    grad_ref, wgrad_ref, turned_ref, faces_ref,
+):
+    slots, chans = first_ref.shape
+    step = pl.program_id(0)
+    unroll = rows_ref.shape[0]
+    half = wgrad_ref.shape[0] // 2
 
     @pl.when(step == 0)
     def _():
-        total_ref[...] = jnp.zeros_like(total_ref)
         gain_term = jnp.zeros((1, chans), jnp.float32)
-        turned_ref[:, :F] = before_ref[...].T
-        turned_ref[:, F + slots :] = after_ref[...].T
+        faces_ref[:, :F] = before_ref[...].T
+        faces_ref[:, F:] = after_ref[...].T
         for start in range(0, slots, B):
             at = slice(start, start + B)
             live = alive(start, B, count_ref[0], chans)
-            masked = (field_ref[at, :].astype(jnp.float32) * live).astype(jnp.bfloat16)
-            turned_ref[:, F + start : F + start + B] = masked.T
             upper = upper_ref[at, :]
             if start == 0:
                 upper = upper + from_prev_ref[...].astype(jnp.float32)
@@ -292,13 +295,34 @@
                 - jnp.mean(grad_unit, axis=-1, keepdims=True)
                 - unit * jnp.mean(grad_unit * unit, axis=-1, keepdims=True)
             )
-            grad_ref[at, :] = (inv_std * centred).astype(jnp.bfloat16)
-        lanes = lax.broadcasted_iota(jnp.int32, (chans, chans), 0)
-        wgrad_ref[wgrad_ref.shape[0] - 1] = jnp.where(
-            lanes == 0, jnp.broadcast_to(gain_term, (chans, chans)), 0.0
-        )
-
-    scatter_step(map_ref, weight_ref, grad_ref, turned_ref, total_ref, wgrad_ref)
+            grad = (inv_std * centred).astype(jnp.bfloat16)
+            grad_ref[at, :] = grad
+            turned_ref[:, at] = grad.T
+        row = lax.broadcasted_iota(jnp.int32, (chans, chans), 0)
+        high = gain_term.astype(jnp.bfloat16).astype(jnp.float32)
+        wgrad_ref[half - 1] = jnp.where(
+            row == 0, high, jnp.where(row == 1, gain_term - high, 0.0)
+        ).astype(jnp.bfloat16)
+        wgrad_ref[2 * half - 1] = jnp.zeros((chans, chans), jnp.bfloat16)
+
+    wide = mm(turned_ref[...], jnp.concatenate([rows_ref[u] for u in range(unroll)], axis=1))
+    edge = mm(faces_ref[...], jnp.concatenate([near_ref[u] for u in range(unroll)], axis=1))
+    for u in range(unroll):
+        at = slice(u * chans, (u + 1) * chans)
+        wgrad_ref[step * unroll + u] = wide[:, at].T.astype(jnp.bfloat16)
+        wgrad_ref[half + step * unroll + u] = (partial_ref[u] + edge[:, at]).astype(jnp.bfloat16)
+
+
+def first_back_body(
+    count_ref, map_ref, grad_ref, weight_ref, own_ref, prev_ref, next_ref, total_ref
+):
+    step = pl.program_id(0)
+
+    @pl.when(step == 0)
+    def _():
+        total_ref[...] = jnp.zeros_like(total_ref)
+
+    scatter_step(map_ref, weight_ref, grad_ref, total_ref)
 
     @pl.when(step == pl.num_programs(0) - 1)
     def _():
@@ -306,26 +330,22 @@
 
 
 def call(body, name, operands, stepped, outputs, scratch):
-    offsets = operands[stepped].shape[0]
+    offsets = operands[stepped[0]].shape[0]
     unroll = 3 if offsets % 3 == 0 else 1
 
-    def whole(shape):
+    def spec(shape, cut):
+        if cut:
+            return pl.BlockSpec((unroll,) + shape[1:], lambda k: (k,) + (0,) * (len(shape) - 1))
         return pl.BlockSpec(shape, lambda k: (0,) * len(shape))
 
-    specs = []
-    for n, operand in enumerate(operands):
-        if n == 0:
-            specs.append(pl.BlockSpec(memory_space=pltpu.SMEM))
-        elif n == stepped:
-            specs.append(pl.BlockSpec((unroll,) + operand.shape[1:], lambda k: (k, 0, 0)))
-        else:
-            specs.append(whole(operand.shape))
+    specs = [pl.BlockSpec(memory_space=pltpu.SMEM)]
+    specs += [spec(o.shape, n in stepped) for n, o in enumerate(operands) if n > 0]
     return pl.pallas_call(
         body,
         grid=(offsets // unroll,),
         in_specs=specs,
-        out_specs=[whole(shape) for shape, _ in outputs],
-        out_shape=[jax.ShapeDtypeStruct(shape, dtype) for shape, dtype in outputs],
+        out_specs=[spec(out[0], len(out) > 2) for out in outputs],
+        out_shape=[jax.ShapeDtypeStruct(out[0], out[1]) for out in outputs],
         scratch_shapes=[pltpu.VMEM(shape, dtype) for shape, dtype in scratch],
         compiler_params=PARAMS,
         name=name,
@@ -342,52 +362,75 @@
     slots, chans = features.shape
     neighbours = kernel_map[0]
     offsets = neighbours.shape[0]
+    devices = lax.axis_size(AXES)
     gain = norm_gain[None, :]
     bf16, f32 = jnp.bfloat16, jnp.float32
     rows16, rows32 = ((slots, chans), bf16), ((slots, chans), f32)
     face16 = ((F, chans), bf16)
     table16 = ((B, slots // B * chans), bf16)
-    turned16 = ((chans, slots + 2 * F), bf16)
+    turned16 = ((chans, slots), bf16)
     total32 = ((slots + 2 * F, chans), f32)
 
     ends = jnp.arange(2 * F, dtype=jnp.int32)[:, None] < counts[0]
     ends_x = (features[: 2 * F].astype(f32) * ends.astype(f32)).astype(bf16)
     before_x, after_x = shifted(ends_x[F:], 1), shifted(ends_x[:F], -1)
     slotted = swap_rows(cotangent)
-    first, hidden = call(
+    first, hidden, rows_x = call(
         first_layer_body, "first_layer",
-        (counts, neighbours, features, before_x, after_x, first_weight, gain), 5,
-        (rows32, rows16), (table16,),
+        (counts, neighbours, features, before_x, after_x, first_weight, gain), (5,),
+        (rows32, rows16, ((offsets, slots, chans), bf16, True)), (table16,),
     )
     before_h, after_h = shifted(hidden[F : 2 * F], 1), shifted(hidden[:F], -1)
-    upper, upper_prev, upper_next, second_term, grad_live = call(
+    upper, upper_prev, upper_next, partial, near, grad_live = call(
         second_back_body, "second_back",
-        (counts, neighbours, send_order, slotted, hidden, before_h, after_h, second_weight), 7,
-        (rows32, face16, face16, ((offsets, chans, chans), f32), rows16), (turned16, total32),
-    )
-    second_grad = lax.psum(second_term, AXES)
+        (counts, neighbours, send_order, slotted, hidden, second_weight), (5,),
+        (rows32, face16, face16, ((offsets, chans, chans), f32, True),
+         ((offsets, 2 * F, chans), bf16, True), rows16),
+        (turned16, total32),
+    )
     from_prev, from_next = shifted(upper_next, 1), shifted(upper_prev, -1)
-    lower, lower_prev, lower_next, first_term = call(
-        first_back_body, "first_back",
-        (counts, neighbours, first, upper, from_prev, from_next, gain, features, before_x,
-         after_x, first_weight), 10,
-        (rows32, face16, face16, ((offsets + 1, chans, chans), f32)),
-        (rows16, turned16, total32),
-    )
-    reduced = lax.psum(first_term, ("tile", "group"))
-    down_prev, down_next = shifted(lower_next, 1), shifted(lower_prev, -1)
+    grad_first, wgrads = call(
+        weights_body, "weights",
+        (counts, first, upper, from_prev, from_next, gain, before_h, after_h, rows_x, near,
+         partial), (8, 9, 10),
+        (rows16, ((2 * (offsets + 1), chans, chans), bf16)), (turned16, ((chans, 2 * F), bf16)),
+    )
+    parts = swap_rows(wgrads.reshape(devices, -1, chans))
+    hidden, grad_first = lax.optimization_barrier((hidden, grad_first))
     (ordered,) = call(
         second_layer_body, "second_layer",
-        (counts, neighbours, send_order, features, hidden, before_h, after_h, second_weight), 7,
-        (rows16,), (rows32, table16),
-    )
-    serial_out = swap_rows(ordered)
+        (counts, neighbours, send_order, features, hidden, before_h, after_h, second_weight),
+        (7,), (rows16,), (rows32, table16),
+    )
+    part = jnp.sum(parts.astype(f32), axis=0).astype(bf16)
+    ordered, part, grad_first = lax.optimization_barrier((ordered, part, grad_first))
+    per_peer = slots // devices
+    both = swap_rows(
+        jnp.concatenate(
+            [
+                ordered.reshape(devices, per_peer, chans),
+                jnp.broadcast_to(part[None], (devices,) + part.shape),
+            ],
+            axis=1,
+        )
+    )
+    serial_out = both[:, :per_peer].reshape(slots, chans)
+    shared = both[:, per_peer:]
+    lower, lower_prev, lower_next = call(
+        first_back_body, "first_back",
+        (counts, neighbours, grad_first, first_weight), (3,),
+        (rows32, face16, face16), (total32,),
+    )
+    down_prev, down_next = shifted(lower_next, 1), shifted(lower_prev, -1)
     live = (jnp.arange(slots, dtype=jnp.int32) < counts[0]).astype(f32)[:, None]
     grad_x = lower + grad_live.astype(f32)
     grad_x = grad_x.at[:F].add(down_prev.astype(f32))
     grad_x = grad_x.at[F : 2 * F].add(down_next.astype(f32))
     grad_features = (grad_x * live).astype(bf16)
-    return (serial_out, grad_features, reduced[:offsets], second_grad, reduced[offsets, 0])
+    shared = shared.reshape(2, offsets + 1, chans, chans)
+    first_grad, second_grad = shared[0, :offsets].astype(f32), shared[1, :offsets].astype(f32)
+    gain_grad = shared[0, offsets, 0].astype(f32) + shared[0, offsets, 1].astype(f32)
+    return (serial_out, grad_features, first_grad, second_grad, gain_grad)
 
 
 def solution(mesh):

time: 481 us -> 275 us (0.57)
  waiting for transfers between devices: 226 us -> 15 us
  between operations: 14.9 us -> 1.51 us
  starting transfers between devices: 37.1 us -> 47 us
  Pallas kernels: 188 us -> 196 us
  local copies, waits for them, and re-layouts: 12.4 us -> 6.37 us
  other arithmetic: 2.31 us -> 8.11 us
    psum x2 -> x0, waiting for transfers between devices: 199 us -> none  [the longest x1 133 us: local(): second_grad = lax.psum(second_term, AXES)]
    all_to_all x2 -> x3, waiting for transfers between devices: 12.2 us -> 1.43 us  [swap_rows(): return lax.all_to_all(rows, AXES, split_axis=0, concat_axis=0, tiled=True)]
    all_to_all x2 -> x3, starting transfers between devices: 15.5 us -> 24.3 us  [swap_rows(): return lax.all_to_all(rows, AXES, split_axis=0, concat_axis=0, tiled=True)]
    pallas_call x4 -> x5, Pallas kernels: 188 us -> 196 us  [call(): pl.pallas_call(body, grid=(offsets // unroll,), in_specs=specs, out_specs...]
  transfers between devices with their start and end apart: 12 -> 11, of which waited for: 8 -> 6; matrix products, arithmetic and copies ran while one was open for 2% -> 2% of each run, Pallas kernels for 18% -> 66%
where the time goes in v3:
time: 275 us; the launch traced here: 274 us
  Pallas kernels  196 us (71%)
  starting transfers between devices  47 us (17%)
  waiting for transfers between devices  15 us (5%)
  other arithmetic  8.11 us (3%)
  local copies, waits for them, and re-layouts  6.37 us (2%)
    pallas_call x5, Pallas kernels, call(): pl.pallas_call(body, grid=(offsets // unroll,), in_specs=specs, out_specs...  196 us
    all_to_all x3, starting transfers between devices, swap_rows(): return lax.all_to_all(rows, AXES, split_axis=0, concat_axis=0, tiled=True)  24.3 us
    ppermute x8, starting transfers between devices, shifted(): lax.ppermute(value, AXES, [(source, source + steps) for source in range(i...  22.7 us
    ppermute x8, waiting for transfers between devices, shifted(): lax.ppermute(value, AXES, [(source, source + steps) for source in range(i...  13.6 us
  transfers between devices with their start and end apart: 11, of which 6 were waited for; matrix products, arithmetic and copies ran while one was open for 2% of the time, Pallas kernels for 66%

profile of v3, /device:TPU:0, one launch (start us, length us, event | category | flops | bytes accessed | tf_op | source)
XLA Modules:
  0.0 274.3 jit_solution(18118765628644402954)
XLA Ops:
  0.6 7.3 %all-to-all-start = ((bf16[32,64,128]{2,1,0:T(8,128)(2,1)}), bf16[32,64,128]{2,1,0:T(8,128)(2,1)S(1)}, u32[]{:S(2)}, u32[]{:S(2)}) async-start(bf16[32,64,128]{2,1,0:T(8,128)(2,1)} %bitcast.34), calls=%async_computation | async-start | bytes 1048576 | tf_op jit(solution)/shard_map/all_to_all | solution.py:356
  9.7 3.7 %collective-permute-start = (bf16[256,128]{1,0:T(8,128)(2,1)S(1)}, bf16[256,128]{1,0:T(8,128)(2,1)S(1)}, u32[]{:S(2)}, u32[]{:S(2)}) collective-permute-start(bf16[256,128]{1,0:T(8,128)(2,1)S(1)} %get-tuple-element.72), channel_id=1, source_target_pairs={{0,1},{1,2},{2,3},{3,4},{4,5},{5,6},{6,7},{7,8},{8,9},{9,10},{10,1... | collective-permute-start | bytes 196616 | tf_op jit(solution)/shard_map/ppermute | solution.py:25
  13.3 1.3 collective-permute-start.1
  14.6 1.7 copy.15
  16.4 3.2 %collective-permute-done.1.after_ref = bf16[256,128]{1,0:T(8,128)(2,1)S(1)} collective-permute-done((bf16[256,128]{1,0:T(8,128)(2,1)S(1)}, bf16[256,128]{1,0:T(8,128)(2,1)S(1)}, u32[]{:S(2)}, u32[]{:S(2)}) %collective-permute-start.1) | collective-permute-done | bytes 65568 | tf_op jit(solution)/shard_map/ppermute | solution.py:25
  20.2 44.8 %first_layer.1 = (f32[2048,128]{1,0:T(8,128)}, bf16[2048,128]{1,0:T(8,128)(2,1)}, bf16[27,2048,128]{2,1,0:T(8,128)(2,1)}) custom-call(s32[1]{0:T(128)} %copy.18.count_ref, s32[27,2048]{1,0:T(8,128)} %bitcast.27, bf16[2048,128]{1,0:T(8,128)(2,1)} %skip_ref.1, bf16[256,128]{1,0:T(8,128)(2,1)} %copy-done.7, bf16[256,128]{1,0:T(8,128)(2,1)} %copy-done.8, ...), custom_call_target="tpu_custom_call" | custom-call | tf_op jit(solution)/shard_map/first_layer/pallas_call | solution.py:343
  65.9 5.5 %collective-permute-start.4 = (bf16[256,128]{1,0:T(8,128)(2,1)S(1)}, bf16[256,128]{1,0:T(8,128)(2,1)S(1)}, u32[]{:S(2)}, u32[]{:S(2)}) collective-permute-start(bf16[256,128]{1,0:T(8,128)(2,1)S(1)} %get-tuple-element.70), channel_id=1, source_target_pairs={{0,1},{1,2},{2,3},{3,4},{4,5},{5,6},{6,7},{7,8},{8,9},{9,10},{10,1... | collective-permute-start | bytes 196616 | tf_op jit(solution)/shard_map/ppermute | solution.py:25
  71.4 1.5 collective-permute-start.5
  73.7 48.3 %second_back.1 = (f32[2048,128]{1,0:T(8,128)}, bf16[256,128]{1,0:T(8,128)(2,1)}, bf16[256,128]{1,0:T(8,128)(2,1)}, f32[27,128,128]{2,1,0:T(8,128)}, bf16[27,512,...) custom-call(s32[1]{0:T(128)} %copy.18.count_ref, s32[27,2048]{1,0:T(8,128)} %bitcast.28, s32[1,2048]{1,0:T(1,128)} %order_ref.3, ...), custom_call_target="tpu_custom_call" | custom-call | tf_op jit(solution)/shard_map/second_back/pallas_call | solution.py:343
  122.0 4.5 %collective-permute-start.2 = (bf16[256,128]{1,0:T(8,128)(2,1)}, bf16[256,128]{1,0:T(8,128)(2,1)S(1)}, u32[]{:S(2)}, u32[]{:S(2)}) collective-permute-start(bf16[256,128]{1,0:T(8,128)(2,1)} %get-tuple-element.51), channel_id=1, source_target_pairs={{0,1},{1,2},{2,3},{3,4},{4,5},{5,6},{6,7},{7,8},{8,9},{9,10},{10,1... | collective-permute-start | bytes 196616 | tf_op jit(solution)/shard_map/ppermute | solution.py:25
  126.5 1.3 collective-permute-start.3
  128.7 4.8 %collective-permute-done.3.from_next_ref = bf16[256,128]{1,0:T(8,128)(2,1)S(1)} collective-permute-done((bf16[256,128]{1,0:T(8,128)(2,1)}, bf16[256,128]{1,0:T(8,128)(2,1)S(1)}, u32[]{:S(2)}, u32[]{:S(2)}) %collective-permute-start.3) | collective-permute-done | bytes 65568 | tf_op jit(solution)/shard_map/ppermute | solution.py:25
  134.2 15.3 %weights.1 = (bf16[2048,128]{1,0:T(8,128)(2,1)}, bf16[56,128,128]{2,1,0:T(8,128)(2,1)}) custom-call(s32[1]{0:T(128)} %copy.18.count_ref, f32[2048,128]{1,0:T(8,128)} %get-tuple-element.49.first_ref, f32[2048,128]{1,0:T(8,128)} %get-tuple-element.50.upper_ref, bf16[256,128]{1,0:T(8,128)(2,1)} %copy-done.5, bf16[256,128]{1,0:T(8,128)(2,1)} %copy-done.6, ...), custom_call_target="tpu_custom_call" | custom-call | tf_op jit(solution)/shard_map/weights/pallas_call | solution.py:343
  149.5 11.4 %all-to-all-start.1 = ((bf16[32,224,128]{2,1,0:T(8,128)(2,1)}), bf16[32,224,128]{2,1,0:T(8,128)(2,1)S(1)}, u32[]{:S(2)}, u32[]{:S(2)}) async-start(bf16[32,224,128]{2,1,0:T(8,128)(2,1)} %bitcast.33), calls=%async_computation.1 | async-start | bytes 3670016 | tf_op jit(solution)/shard_map/all_to_all | solution.py:356
  161.0 44.2 %second_layer.1 = bf16[2048,128]{1,0:T(8,128)(2,1)} custom-call(s32[1]{0:T(128)} %copy.18.count_ref, s32[27,2048]{1,0:T(8,128)} %bitcast.29, s32[1,2048]{1,0:T(1,128)} %order_ref.3, bf16[2048,128]{1,0:T(8,128)(2,1)} %skip_ref.1, bf16[2048,128]{1,0:T(8,128)(2,1)} %get-tuple-element.57.field_ref, bf16[256,128]{1,0:T(8,128)(2,1)} %copy-done.3, ...), custom_call_target="tpu_custom_call" | custom-call | tf_op jit(solution)/shard_map/second_layer/pallas_call | solution.py:343
  206.2 1.6 pad_maximum_fusion
  207.8 5.6 %all-to-all-start.2 = ((bf16[32,288,128]{2,1,0:T(8,128)(2,1)}), bf16[32,288,128]{2,1,0:T(8,128)(2,1)S(1)}, u32[]{:S(2)}, u32[]{:S(2)}) async-start(bf16[32,288,128]{2,1,0:T(8,128)(2,1)} %pad_maximum_fusion), calls=%async_computation.2 | async-start | bytes 4718592 | tf_op jit(solution)/shard_map/all_to_all | solution.py:356
  213.4 43.6 %first_back.1 = (f32[2048,128]{1,0:T(8,128)}, bf16[256,128]{1,0:T(8,128)(2,1)}, bf16[256,128]{1,0:T(8,128)(2,1)}) custom-call(s32[1]{0:T(128)} %copy.18.count_ref, s32[27,2048]{1,0:T(8,128)} %bitcast.30, bf16[2048,128]{1,0:T(8,128)(2,1)} %get-tuple-element.62.grad_ref, bf16[27,128,128]{2,1,0:T(8,128)(2,1)} %weight_ref.7), custom_call_target="tpu_custom_call" | custom-call | tf_op jit(solution)/shard_map/first_back/pallas_call | solution.py:343
  257.0 3.7 %collective-permute-start.6 = (bf16[256,128]{1,0:T(8,128)(2,1)}, bf16[256,128]{1,0:T(8,128)(2,1)S(1)}, u32[]{:S(2)}, u32[]{:S(2)}) collective-permute-start(bf16[256,128]{1,0:T(8,128)(2,1)} %get-tuple-element.65), channel_id=1, source_target_pairs={{0,1},{1,2},{2,3},{3,4},{4,5},{5,6},{6,7},{7,8},{8,9},{9,10},{10,1... | collective-permute-start | bytes 196616 | tf_op jit(solution)/shard_map/ppermute | solution.py:25
  260.7 1.3 collective-permute-start.7
  262.0 1.3 convert_add_fusion
  263.7 4.4 %collective-permute-done.7 = bf16[256,128]{1,0:T(8,128)(2,1)S(1)} collective-permute-done((bf16[256,128]{1,0:T(8,128)(2,1)}, bf16[256,128]{1,0:T(8,128)(2,1)S(1)}, u32[]{:S(2)}, u32[]{:S(2)}) %collective-permute-start.7) | collective-permute-done | bytes 65568 | tf_op jit(solution)/shard_map/ppermute | solution.py:25
  269.2 1.4 all-to-all-done.2
  270.7 2.2 fusion
  (38 shorter events, 8.9 us)
Async XLA Ops:
  0.6 72.2 %all-to-all-start = ((bf16[32,64,128]{2,1,0:T(8,128)(2,1)}), bf16[32,64,128]{2,1,0:T(8,128)(2,1)S(1)}, u32[]{:S(2)}, u32[]{:S(2)}) async-start(bf16[32,64,128]{2,1,0:T(8,128)(2,1)} %bitcast.34), calls=%async_computation | async-start | bytes 1048576 | tf_op jit(solution)/shard_map/all_to_all | solution.py:356
  9.7 6.7 %collective-permute-start = (bf16[256,128]{1,0:T(8,128)(2,1)S(1)}, bf16[256,128]{1,0:T(8,128)(2,1)S(1)}, u32[]{:S(2)}, u32[]{:S(2)}) collective-permute-start(bf16[256,128]{1,0:T(8,128)(2,1)S(1)} %get-tuple-element.72), channel_id=1, source_target_pairs={{0,1},{1,2},{2,3},{3,4},{4,5},{5,6},{6,7},{7,8},{8,9},{9,10},{10,1... | collective-permute-start | bytes 196616 | tf_op jit(solution)/shard_map/ppermute | solution.py:25
  13.3 6.2 %collective-permute-start.1 = (bf16[256,128]{1,0:T(8,128)(2,1)S(1)}, bf16[256,128]{1,0:T(8,128)(2,1)S(1)}, u32[]{:S(2)}, u32[]{:S(2)}) collective-permute-start(bf16[256,128]{1,0:T(8,128)(2,1)S(1)} %get-tuple-element.71), channel_id=1, source_target_pairs={{1,0},{2,1},{3,2},{4,3},{5,4},{6,5},{7,6},{8,7},{9,8},{10,9},{11,1... | collective-permute-start | bytes 196616 | tf_op jit(solution)/shard_map/ppermute | solution.py:25
  16.4 3.2 %copy-start.7 = (bf16[256,128]{1,0:T(8,128)(2,1)}, bf16[256,128]{1,0:T(8,128)(2,1)S(1)}, u32[]{:S(2)}) copy-start(bf16[256,128]{1,0:T(8,128)(2,1)S(1)} %collective-permute-done.before_ref) | copy-start | bytes 196612
  19.6 0.6 copy-start.8
  65.9 61.9 %collective-permute-start.4 = (bf16[256,128]{1,0:T(8,128)(2,1)S(1)}, bf16[256,128]{1,0:T(8,128)(2,1)S(1)}, u32[]{:S(2)}, u32[]{:S(2)}) collective-permute-start(bf16[256,128]{1,0:T(8,128)(2,1)S(1)} %get-tuple-element.70), channel_id=1, source_target_pairs={{0,1},{1,2},{2,3},{3,4},{4,5},{5,6},{6,7},{7,8},{8,9},{9,10},{10,1... | collective-permute-start | bytes 196616 | tf_op jit(solution)/shard_map/ppermute | solution.py:25
  71.4 56.5 %collective-permute-start.5 = (bf16[256,128]{1,0:T(8,128)(2,1)S(1)}, bf16[256,128]{1,0:T(8,128)(2,1)S(1)}, u32[]{:S(2)}, u32[]{:S(2)}) collective-permute-start(bf16[256,128]{1,0:T(8,128)(2,1)S(1)} %get-tuple-element.69), channel_id=1, source_target_pairs={{1,0},{2,1},{3,2},{4,3},{5,4},{6,5},{7,6},{8,7},{9,8},{10,9},{11,1... | collective-permute-start | bytes 196616 | tf_op jit(solution)/shard_map/ppermute | solution.py:25
  72.9 0.8 copy-start
  122.0 6.7 %collective-permute-start.2 = (bf16[256,128]{1,0:T(8,128)(2,1)}, bf16[256,128]{1,0:T(8,128)(2,1)S(1)}, u32[]{:S(2)}, u32[]{:S(2)}) collective-permute-start(bf16[256,128]{1,0:T(8,128)(2,1)} %get-tuple-element.51), channel_id=1, source_target_pairs={{0,1},{1,2},{2,3},{3,4},{4,5},{5,6},{6,7},{7,8},{8,9},{9,10},{10,1... | collective-permute-start | bytes 196616 | tf_op jit(solution)/shard_map/ppermute | solution.py:25
  126.5 7.0 %collective-permute-start.3 = (bf16[256,128]{1,0:T(8,128)(2,1)}, bf16[256,128]{1,0:T(8,128)(2,1)S(1)}, u32[]{:S(2)}, u32[]{:S(2)}) collective-permute-start(bf16[256,128]{1,0:T(8,128)(2,1)} %get-tuple-element.52), channel_id=1, source_target_pairs={{1,0},{2,1},{3,2},{4,3},{5,4},{6,5},{7,6},{8,7},{9,8},{10,9},{11,1... | collective-permute-start | bytes 196616 | tf_op jit(solution)/shard_map/ppermute | solution.py:25
  127.8 5.7 %copy-start.3 = (bf16[256,128]{1,0:T(8,128)(2,1)}, bf16[256,128]{1,0:T(8,128)(2,1)S(1)}, u32[]{:S(2)}) copy-start(bf16[256,128]{1,0:T(8,128)(2,1)S(1)} %collective-permute-done.4.before_ref) | copy-start | bytes 196612
  127.9 5.7 %copy-start.4 = (bf16[256,128]{1,0:T(8,128)(2,1)}, bf16[256,128]{1,0:T(8,128)(2,1)S(1)}, u32[]{:S(2)}) copy-start(bf16[256,128]{1,0:T(8,128)(2,1)S(1)} %collective-permute-done.5.after_ref) | copy-start | bytes 196612
  128.7 4.8 %copy-start.5 = (bf16[256,128]{1,0:T(8,128)(2,1)}, bf16[256,128]{1,0:T(8,128)(2,1)S(1)}, u32[]{:S(2)}) copy-start(bf16[256,128]{1,0:T(8,128)(2,1)S(1)} %collective-permute-done.2.from_prev_ref) | copy-start | bytes 196612
  133.6 0.6 copy-start.6
  149.5 55.7 %all-to-all-start.1 = ((bf16[32,224,128]{2,1,0:T(8,128)(2,1)}), bf16[32,224,128]{2,1,0:T(8,128)(2,1)S(1)}, u32[]{:S(2)}, u32[]{:S(2)}) async-start(bf16[32,224,128]{2,1,0:T(8,128)(2,1)} %bitcast.33), calls=%async_computation.1 | async-start | bytes 3670016 | tf_op jit(solution)/shard_map/all_to_all | solution.py:356
  205.1 1.0 copy-start.1
  207.8 62.8 %all-to-all-start.2 = ((bf16[32,288,128]{2,1,0:T(8,128)(2,1)}), bf16[32,288,128]{2,1,0:T(8,128)(2,1)S(1)}, u32[]{:S(2)}, u32[]{:S(2)}) async-start(bf16[32,288,128]{2,1,0:T(8,128)(2,1)} %pad_maximum_fusion), calls=%async_computation.2 | async-start | bytes 4718592 | tf_op jit(solution)/shard_map/all_to_all | solution.py:356
  213.4 48.6 %copy-start.2 = (bf16[2048,128]{1,0:T(8,128)(2,1)S(1)}, bf16[2048,128]{1,0:T(8,128)(2,1)}, u32[]{:S(2)}) copy-start(bf16[2048,128]{1,0:T(8,128)(2,1)} %get-tuple-element.64) | copy-start | bytes 1572868
  257.0 6.6 %collective-permute-start.6 = (bf16[256,128]{1,0:T(8,128)(2,1)}, bf16[256,128]{1,0:T(8,128)(2,1)S(1)}, u32[]{:S(2)}, u32[]{:S(2)}) collective-permute-start(bf16[256,128]{1,0:T(8,128)(2,1)} %get-tuple-element.65), channel_id=1, source_target_pairs={{0,1},{1,2},{2,3},{3,4},{4,5},{5,6},{6,7},{7,8},{8,9},{9,10},{10,1... | collective-permute-start | bytes 196616 | tf_op jit(solution)/shard_map/ppermute | solution.py:25
  260.7 7.4 %collective-permute-start.7 = (bf16[256,128]{1,0:T(8,128)(2,1)}, bf16[256,128]{1,0:T(8,128)(2,1)S(1)}, u32[]{:S(2)}, u32[]{:S(2)}) collective-permute-start(bf16[256,128]{1,0:T(8,128)(2,1)} %get-tuple-element.66), channel_id=1, source_target_pairs={{1,0},{2,1},{3,2},{4,3},{5,4},{6,5},{7,6},{8,7},{9,8},{10,9},{11,1... | collective-permute-start | bytes 196616 | tf_op jit(solution)/shard_map/ppermute | solution.py:25

commit v4 on v3

--- a/solution.py
+++ b/solution.py
@@ -153,7 +153,7 @@
 
 
 def second_layer_body(
-    count_ref, map_ref, order_ref, skip_ref, field_ref, before_ref, after_ref, weight_ref,
+    count_ref, map_ref, order_ref, skip_ref, field_ref, below_ref, above_ref, weight_ref,
     serial_ref, second_ref, table_ref,
 ):
     slots, chans = field_ref.shape
@@ -164,7 +164,8 @@
         second_ref[...] = jnp.zeros_like(second_ref)
         load_table(table_ref, field_ref, 0, slots, chans)
 
-    gather_step(map_ref, before_ref, after_ref, weight_ref, second_ref, table_ref, slots, chans)
+    faces = (below_ref.at[pl.ds(F, F), :], above_ref.at[pl.ds(F, F), :])
+    gather_step(map_ref, *faces, weight_ref, second_ref, table_ref, slots, chans)
 
     @pl.when(step == pl.num_programs(0) - 1)
     def _():
@@ -182,68 +183,67 @@
             )
 
 
-def scatter_step(map_ref, weight_ref, grad_ref, total_ref, near_ref=None, turned_ref=None, wgrad_ref=None):
-    slots, chans = grad_ref.shape
-    groups = slots // B
+def edge_step(map_ref, weight_ref, grad_ref, edge_ref, near_ref=None):
+    chans = grad_ref.shape[1]
+    slots = grad_ref.shape[0]
     step = pl.program_id(0)
     unroll = weight_ref.shape[0]
-    near, own = [], []
-    for u in range(unroll):
-        row = map_ref[pl.ds(step * unroll + u, 1), :]
-        entry = lane_replicated(row)
-        grad = grad_ref[...].astype(jnp.float32)
-        own.append(drop(row - F, entry - F, grad, groups).astype(jnp.bfloat16))
-        faces = []
-        for side in range(2):
-            at = slice(side * F, (side + 1) * F)
-            crossing = jnp.where(side_mask(entry[at], side, slots), grad[at], 0.0)
-            faces.append(
-                mm(onehot_cols(row[:, at] & (F - 1), F), crossing.astype(jnp.bfloat16)).astype(
+    back = jnp.concatenate([weight_ref[u] for u in range(unroll)], axis=1)
+    for side in range(2):
+        at = slice(side * F, (side + 1) * F)
+        grad = grad_ref[at, :].astype(jnp.float32)
+        sums = []
+        for u in range(unroll):
+            row = map_ref[pl.ds(step * unroll + u, 1), at]
+            crossing = jnp.where(side_mask(lane_replicated(row), side, slots), grad, 0.0)
+            sums.append(
+                mm(onehot_cols(row & (F - 1), F), crossing.astype(jnp.bfloat16)).astype(
                     jnp.bfloat16
                 )
             )
             if near_ref is not None:
-                near_ref[u, at, :] = faces[-1]
-        near.append(faces)
+                near_ref[u, at, :] = sums[-1]
+        edge_ref[at, :] += lax.dot_general(
+            jnp.concatenate(sums, axis=1), back, NT, preferred_element_type=jnp.float32
+        )
+
+
+def scatter_step(map_ref, weight_ref, grad_ref, total_ref, turned_ref=None, wgrad_ref=None):
+    slots, chans = grad_ref.shape
+    groups = slots // B
+    step = pl.program_id(0)
+    unroll = weight_ref.shape[0]
+    own = []
+    for u in range(unroll):
+        row = map_ref[pl.ds(step * unroll + u, 1), :]
+        grad = grad_ref[...].astype(jnp.float32)
+        own.append(drop(row - F, lane_replicated(row) - F, grad, groups).astype(jnp.bfloat16))
     back = jnp.concatenate([weight_ref[u] for u in range(unroll)], axis=1)
     wide = None
-    starts = [0] + [F + a * B for a in range(groups)] + [F + slots]
-    for n, start in enumerate(starts):
-        inside = 0 < n <= groups
-        if inside:
-            a = n - 1
-            piece = [own[u][:, a * chans : (a + 1) * chans] for u in range(unroll)]
-        else:
-            piece = [near[u][0 if n == 0 else 1] for u in range(unroll)]
-        piece = jnp.concatenate(piece, axis=1)
-        at = slice(start, start + piece.shape[0])
+    for a in range(groups):
+        piece = jnp.concatenate(
+            [own[u][:, a * chans : (a + 1) * chans] for u in range(unroll)], axis=1
+        )
+        at = slice(a * B, (a + 1) * B)
         total_ref[at, :] += lax.dot_general(piece, back, NT, preferred_element_type=jnp.float32)
-        if inside and wgrad_ref is not None:
-            term = mm(turned_ref[:, a * B : (a + 1) * B], piece)
+        if wgrad_ref is not None:
+            term = mm(turned_ref[:, at], piece)
             wide = term if wide is None else wide + term
     if wgrad_ref is not None:
         for u in range(unroll):
             wgrad_ref[u] = wide[:, u * chans : (u + 1) * chans]
 
 
-def give_back(total_ref, own_ref, prev_ref, next_ref):
-    slots = own_ref.shape[0]
-    own_ref[...] = total_ref[F : F + slots, :]
-    prev_ref[...] = total_ref[:F, :].astype(jnp.bfloat16)
-    next_ref[...] = total_ref[F + slots :, :].astype(jnp.bfloat16)
-
-
-def second_back_body(
-    count_ref, map_ref, order_ref, slotted_ref, field_ref, weight_ref,
-    own_ref, prev_ref, next_ref, wgrad_ref, near_ref, grad_ref, turned_ref, total_ref,
-):
-    slots, chans = field_ref.shape
-    step = pl.program_id(0)
-
-    @pl.when(step == 0)
-    def _():
-        total_ref[...] = jnp.zeros_like(total_ref)
-        turned_ref[...] = field_ref[...].T
+def second_edges_body(
+    count_ref, map_ref, order_ref, slotted_ref, ends_ref, weight_ref,
+    grad_ref, near_ref, up_ref, down_ref, edge_ref,
+):
+    slots, chans = slotted_ref.shape
+    step = pl.program_id(0)
+
+    @pl.when(step == 0)
+    def _():
+        edge_ref[...] = jnp.zeros_like(edge_ref)
         order = order_ref[...]
         placed = drop(
             order, lane_replicated(order), slotted_ref[...].astype(jnp.float32), slots // B
@@ -254,17 +254,33 @@
                 placed[:, a * chans : (a + 1) * chans] * live
             ).astype(jnp.bfloat16)
 
-    scatter_step(map_ref, weight_ref, grad_ref, total_ref, near_ref, turned_ref, wgrad_ref)
+    edge_step(map_ref, weight_ref, grad_ref, edge_ref, near_ref)
 
     @pl.when(step == pl.num_programs(0) - 1)
     def _():
-        give_back(total_ref, own_ref, prev_ref, next_ref)
+        up_ref[:F, :] = edge_ref[F:, :].astype(jnp.bfloat16)
+        up_ref[F:, :] = ends_ref[F:, :]
+        down_ref[:F, :] = edge_ref[:F, :].astype(jnp.bfloat16)
+        down_ref[F:, :] = ends_ref[:F, :]
+
+
+def second_back_body(
+    count_ref, map_ref, grad_ref, field_ref, weight_ref, total_ref, wgrad_ref, turned_ref
+):
+    step = pl.program_id(0)
+
+    @pl.when(step == 0)
+    def _():
+        total_ref[...] = jnp.zeros_like(total_ref)
+        turned_ref[...] = field_ref[...].T
+
+    scatter_step(map_ref, weight_ref, grad_ref, total_ref, turned_ref, wgrad_ref)
 
 
 def weights_body(
-    count_ref, first_ref, upper_ref, from_prev_ref, from_next_ref, gain_ref,
-    before_ref, after_ref, rows_ref, near_ref, partial_ref,
-    grad_ref, wgrad_ref, turned_ref, faces_ref,
+    count_ref, map_ref, first_ref, upper_ref, below_ref, above_ref, gain_ref,
+    weight_ref, rows_ref, near_ref, partial_ref,
+    grad_ref, wgrad_ref, up_ref, down_ref, turned_ref, faces_ref, edge_ref,
 ):
     slots, chans = first_ref.shape
     step = pl.program_id(0)
@@ -273,17 +289,18 @@
 
     @pl.when(step == 0)
     def _():
+        edge_ref[...] = jnp.zeros_like(edge_ref)
         gain_term = jnp.zeros((1, chans), jnp.float32)
-        faces_ref[:, :F] = before_ref[...].T
-        faces_ref[:, F:] = after_ref[...].T
+        faces_ref[:, :F] = below_ref[F:, :].T
+        faces_ref[:, F:] = above_ref[F:, :].T
         for start in range(0, slots, B):
             at = slice(start, start + B)
             live = alive(start, B, count_ref[0], chans)
             upper = upper_ref[at, :]
             if start == 0:
-                upper = upper + from_prev_ref[...].astype(jnp.float32)
+                upper = upper + below_ref[:F, :].astype(jnp.float32)
             if start == F:
-                upper = upper + from_next_ref[...].astype(jnp.float32)
+                upper = upper + above_ref[:F, :].astype(jnp.float32)
             unit, inv_std, normed, bent = normalise(first_ref[at, :], gain_ref[...])
             inner = GELU_SCALE * (1.0 + 3.0 * GELU_CUBIC * (normed * normed))
             slope = 0.5 * (1.0 + bent) + 0.5 * normed * (1.0 - bent * bent) * inner
@@ -305,6 +322,7 @@
         ).astype(jnp.bfloat16)
         wgrad_ref[2 * half - 1] = jnp.zeros((chans, chans), jnp.bfloat16)
 
+    edge_step(map_ref, weight_ref, grad_ref, edge_ref)
     wide = mm(turned_ref[...], jnp.concatenate([rows_ref[u] for u in range(unroll)], axis=1))
     edge = mm(faces_ref[...], jnp.concatenate([near_ref[u] for u in range(unroll)], axis=1))
     for u in range(unroll):
@@ -312,26 +330,38 @@
         wgrad_ref[step * unroll + u] = wide[:, at].T.astype(jnp.bfloat16)
         wgrad_ref[half + step * unroll + u] = (partial_ref[u] + edge[:, at]).astype(jnp.bfloat16)
 
+    @pl.when(step == pl.num_programs(0) - 1)
+    def _():
+        up_ref[...] = edge_ref[F:, :].astype(jnp.bfloat16)
+        down_ref[...] = edge_ref[:F, :].astype(jnp.bfloat16)
+
 
 def first_back_body(
-    count_ref, map_ref, grad_ref, weight_ref, own_ref, prev_ref, next_ref, total_ref
-):
-    step = pl.program_id(0)
-
-    @pl.when(step == 0)
-    def _():
-        total_ref[...] = jnp.zeros_like(total_ref)
+    count_ref, map_ref, grad_ref, top_ref, from_prev_ref, from_next_ref, weight_ref,
+    out_ref, total_ref,
+):
+    slots, chans = grad_ref.shape
+    step = pl.program_id(0)
+
+    @pl.when(step == 0)
+    def _():
+        total_ref[...] = top_ref[...].astype(jnp.float32)
+        total_ref[:F, :] += from_prev_ref[...].astype(jnp.float32)
+        total_ref[F : 2 * F, :] += from_next_ref[...].astype(jnp.float32)
 
     scatter_step(map_ref, weight_ref, grad_ref, total_ref)
 
     @pl.when(step == pl.num_programs(0) - 1)
     def _():
-        give_back(total_ref, own_ref, prev_ref, next_ref)
-
-
-def call(body, name, operands, stepped, outputs, scratch):
+        live = alive(0, slots, count_ref[0], chans)
+        out_ref[...] = (total_ref[...] * live).astype(jnp.bfloat16)
+
+
+def call(body, name, operands, stepped, outputs, scratch, together=3, dense=True):
     offsets = operands[stepped[0]].shape[0]
-    unroll = 3 if offsets % 3 == 0 else 1
+    unroll = together if offsets % together == 0 else 1
+    slots, chans = operands[1].shape[1], operands[stepped[0]].shape[2]
+    width = slots if dense else 4 * chans
 
     def spec(shape, cut):
         if cut:
@@ -348,6 +378,11 @@
         out_shape=[jax.ShapeDtypeStruct(out[0], out[1]) for out in outputs],
         scratch_shapes=[pltpu.VMEM(shape, dtype) for shape, dtype in scratch],
         compiler_params=PARAMS,
+        cost_estimate=pl.CostEstimate(
+            flops=7 * offsets * slots * width * chans // 2,
+            transcendentals=0,
+            bytes_accessed=4 * slots * chans,
+        ),
         name=name,
     )(*operands)
 
@@ -369,7 +404,6 @@
     face16 = ((F, chans), bf16)
     table16 = ((B, slots // B * chans), bf16)
     turned16 = ((chans, slots), bf16)
-    total32 = ((slots + 2 * F, chans), f32)
 
     ends = jnp.arange(2 * F, dtype=jnp.int32)[:, None] < counts[0]
     ends_x = (features[: 2 * F].astype(f32) * ends.astype(f32)).astype(bf16)
@@ -380,26 +414,32 @@
         (counts, neighbours, features, before_x, after_x, first_weight, gain), (5,),
         (rows32, rows16, ((offsets, slots, chans), bf16, True)), (table16,),
     )
-    before_h, after_h = shifted(hidden[F : 2 * F], 1), shifted(hidden[:F], -1)
-    upper, upper_prev, upper_next, partial, near, grad_live = call(
+    edge32 = ((2 * F, chans), f32)
+    ends16 = ((2 * F, chans), bf16)
+    grad_live, near, upper_up, upper_down = call(
+        second_edges_body, "second_edges",
+        (counts, neighbours, send_order, slotted, hidden[: 2 * F], second_weight), (5,),
+        (rows16, ((offsets, 2 * F, chans), bf16, True), ends16, ends16), (edge32,), 9, False,
+    )
+    below, above = shifted(upper_up, 1), shifted(upper_down, -1)
+    upper, partial = call(
         second_back_body, "second_back",
-        (counts, neighbours, send_order, slotted, hidden, second_weight), (5,),
-        (rows32, face16, face16, ((offsets, chans, chans), f32, True),
-         ((offsets, 2 * F, chans), bf16, True), rows16),
-        (turned16, total32),
-    )
-    from_prev, from_next = shifted(upper_next, 1), shifted(upper_prev, -1)
-    grad_first, wgrads = call(
+        (counts, neighbours, grad_live, hidden, second_weight), (4,),
+        (rows32, ((offsets, chans, chans), f32, True)), (turned16,),
+    )
+    grad_first, wgrads, lower_up, lower_down = call(
         weights_body, "weights",
-        (counts, first, upper, from_prev, from_next, gain, before_h, after_h, rows_x, near,
-         partial), (8, 9, 10),
-        (rows16, ((2 * (offsets + 1), chans, chans), bf16)), (turned16, ((chans, 2 * F), bf16)),
-    )
+        (counts, neighbours, first, upper, below, above, gain, first_weight, rows_x, near,
+         partial), (7, 8, 9, 10),
+        (rows16, ((2 * (offsets + 1), chans, chans), bf16), face16, face16),
+        (turned16, ((chans, 2 * F), bf16), edge32), 3, False,
+    )
+    from_prev, from_next = shifted(lower_up, 1), shifted(lower_down, -1)
     parts = swap_rows(wgrads.reshape(devices, -1, chans))
     hidden, grad_first = lax.optimization_barrier((hidden, grad_first))
     (ordered,) = call(
         second_layer_body, "second_layer",
-        (counts, neighbours, send_order, features, hidden, before_h, after_h, second_weight),
+        (counts, neighbours, send_order, features, hidden, below, above, second_weight),
         (7,), (rows16,), (rows32, table16),
     )
     part = jnp.sum(parts.astype(f32), axis=0).astype(bf16)
@@ -416,17 +456,11 @@
     )
     serial_out = both[:, :per_peer].reshape(slots, chans)
     shared = both[:, per_peer:]
-    lower, lower_prev, lower_next = call(
+    (grad_features,) = call(
         first_back_body, "first_back",
-        (counts, neighbours, grad_first, first_weight), (3,),
-        (rows32, face16, face16), (total32,),
-    )
-    down_prev, down_next = shifted(lower_next, 1), shifted(lower_prev, -1)
-    live = (jnp.arange(slots, dtype=jnp.int32) < counts[0]).astype(f32)[:, None]
-    grad_x = lower + grad_live.astype(f32)
-    grad_x = grad_x.at[:F].add(down_prev.astype(f32))
-    grad_x = grad_x.at[F : 2 * F].add(down_next.astype(f32))
-    grad_features = (grad_x * live).astype(bf16)
+        (counts, neighbours, grad_first, grad_live, from_prev, from_next, first_weight), (6,),
+        (rows16,), (rows32,),
+    )
     shared = shared.reshape(2, offsets + 1, chans, chans)
     first_grad, second_grad = shared[0, :offsets].astype(f32), shared[1, :offsets].astype(f32)
     gain_grad = shared[0, offsets, 0].astype(f32) + shared[0, offsets, 1].astype(f32)

time: 275 us -> 268 us (0.975)
  starting transfers between devices: 47 us -> 39.3 us
    all_to_all x3, waiting for transfers between devices: 1.43 us -> 15.4 us  [swap_rows(): return lax.all_to_all(rows, AXES, split_axis=0, concat_axis=0, tiled=True)]
    ppermute x8 -> x6, waiting for transfers between devices: 13.6 us -> 0.02 us  [shifted(): lax.ppermute(value, AXES, [(source, source + steps) for source in range(i...]
    ppermute x8 -> x6, starting transfers between devices: 22.7 us -> 17.1 us  [shifted(): lax.ppermute(value, AXES, [(source, source + steps) for source in range(i...]
    unnamed x19 -> x21, local copies, waits for them, and re-layouts: 4.26 us -> 5.6 us
    pallas_call x5 -> x6, Pallas kernels: 196 us -> 197 us  [call(): pl.pallas_call(body, grid=(offsets // unroll,), in_specs=specs, out_specs...]
  transfers between devices with their start and end apart: 11 -> 9, of which waited for: 6 -> 1; matrix products, arithmetic and copies ran while one was open for 2% -> 2% of each run, Pallas kernels for 66% -> 64%
where the time goes in v4:
time: 268 us; the launch traced here: 267 us
  Pallas kernels  197 us (74%)
  starting transfers between devices  39.3 us (15%)
  waiting for transfers between devices  15.4 us (6%)
  local copies, waits for them, and re-layouts  8.4 us (3%)
  other arithmetic  5.61 us (2%)
    pallas_call x6, Pallas kernels, call(): pl.pallas_call(body, grid=(offsets // unroll,), in_specs=specs, out_specs...  197 us
    all_to_all x3, starting transfers between devices, swap_rows(): return lax.all_to_all(rows, AXES, split_axis=0, concat_axis=0, tiled=True)  22.2 us
    ppermute x6, starting transfers between devices, shifted(): lax.ppermute(value, AXES, [(source, source + steps) for source in range(i...  17.1 us
    all_to_all x3, waiting for transfers between devices, swap_rows(): return lax.all_to_all(rows, AXES, split_axis=0, concat_axis=0, tiled=True)  15.4 us
    unnamed x21, local copies, waits for them, and re-layouts  5.6 us
  transfers between devices with their start and end apart: 9, of which 1 were waited for; matrix products, arithmetic and copies ran while one was open for 2% of the time, Pallas kernels for 64%

profile of v4, /device:TPU:0, one launch (start us, length us, event | category | flops | bytes accessed | tf_op | source)
XLA Modules:
  0.0 266.9 jit_solution(10903272996225246188)
XLA Ops:
  1.3 1.0 multiply_convert_fusion
  2.4 1.3 collective-permute-start.1
  3.7 5.5 %collective-permute-start = (bf16[256,128]{1,0:T(8,128)(2,1)S(1)}, bf16[256,128]{1,0:T(8,128)(2,1)S(1)}, u32[]{:S(2)}, u32[]{:S(2)}) collective-permute-start(bf16[256,128]{1,0:T(8,128)(2,1)S(1)} %get-tuple-element.44), channel_id=1, source_target_pairs={{0,1},{1,2},{2,3},{3,4},{4,5},{5,6},{6,7},{7,8},{8,9},{9,10},{10,1... | collective-permute-start | bytes 196616 | tf_op jit(solution)/shard_map/ppermute | solution.py:25
  9.1 8.8 %all-to-all-start = ((bf16[32,64,128]{2,1,0:T(8,128)(2,1)}), bf16[32,64,128]{2,1,0:T(8,128)(2,1)S(1)}, u32[]{:S(2)}, u32[]{:S(2)}) async-start(bf16[32,64,128]{2,1,0:T(8,128)(2,1)} %bitcast.28), calls=%async_computation | async-start | bytes 1048576 | tf_op jit(solution)/shard_map/all_to_all | solution.py:391
  17.9 1.7 copy.15
  20.3 44.8 %first_layer.1 = (f32[2048,128]{1,0:T(8,128)}, bf16[2048,128]{1,0:T(8,128)(2,1)}, bf16[27,2048,128]{2,1,0:T(8,128)(2,1)}) custom-call(s32[1]{0:T(128)} %copy.16.count_ref, s32[27,2048]{1,0:T(8,128)} %bitcast.31, bf16[2048,128]{1,0:T(8,128)(2,1)} %skip_ref.1, bf16[256,128]{1,0:T(8,128)(2,1)} %copy-done.9, bf16[256,128]{1,0:T(8,128)(2,1)} %copy-done.8, ...), custom_call_target="tpu_custom_call" | custom-call | flops 50734301184 | bytes 1048576 | tf_op jit(solution)/shard_map/first_layer/pallas_call | solution.py:373
  65.1 1.6 slice.33.ends_ref
  66.7 0.8 copy-done.1
  67.5 8.1 %second_edges.1 = (bf16[2048,128]{1,0:T(8,128)(2,1)}, bf16[27,512,128]{2,1,0:T(8,128)(2,1)}, bf16[512,128]{1,0:T(8,128)(2,1)}, bf16[512,128]{1,0:T(8,128)(2,1)}) custom-call(s32[1]{0:T(128)} %copy.16.count_ref, s32[27,2048]{1,0:T(8,128)} %bitcast.32, s32[1,2048]{1,0:T(1,128)} %order_ref.3, bf16[2048,128]{1,0:T(8,128)(2,1)} %bitcast.29, ...), custom_call_target="tpu_custom_call" | custom-call | flops 12683575296 | bytes 1048576 | tf_op jit(solution)/shard_map/second_edges/pallas_call | solution.py:373
  75.6 3.7 %collective-permute-start.2 = (bf16[512,128]{1,0:T(8,128)(2,1)}, bf16[512,128]{1,0:T(8,128)(2,1)S(1)}, u32[]{:S(2)}, u32[]{:S(2)}) collective-permute-start(bf16[512,128]{1,0:T(8,128)(2,1)} %get-tuple-element.27), channel_id=1, source_target_pairs={{0,1},{1,2},{2,3},{3,4},{4,5},{5,6},{6,7},{7,8},{8,9},{9,10},{10,1... | collective-permute-start | bytes 393224 | tf_op jit(solution)/shard_map/ppermute | solution.py:25
  79.3 1.5 collective-permute-start.3
  80.8 41.6 %second_back.1 = (f32[2048,128]{1,0:T(8,128)}, f32[27,128,128]{2,1,0:T(8,128)}) custom-call(s32[1]{0:T(128)} %copy.16.count_ref, s32[27,2048]{1,0:T(8,128)} %bitcast.33, bf16[2048,128]{1,0:T(8,128)(2,1)} %get-tuple-element.25.grad_ref.top_ref, bf16[2048,128]{1,0:T(8,128)(2,1)} %get-tuple-element.33.field_ref, bf16[27,128,128]{2,1,0:T(8,128)(2,1)} %weight_ref.10), custom_call_target="tpu_custom_call" | custom-call | flops 50734301184 | bytes 1048576 | tf_op jit(solution)/shard_map/second_back/pallas_call | solution.py:373
  123.1 18.8 %weights.1 = (bf16[2048,128]{1,0:T(8,128)(2,1)}, bf16[56,128,128]{2,1,0:T(8,128)(2,1)}, bf16[256,128]{1,0:T(8,128)(2,1)}, bf16[256,128]{1,0:T(8,128)(2,1)}) custom-call(s32[1]{0:T(128)} %copy.16.count_ref, s32[27,2048]{1,0:T(8,128)} %bitcast.34, f32[2048,128]{1,0:T(8,128)} %get-tuple-element.24.first_ref, f32[2048,128]{1,0:T(8,128)} %get-tuple-element.26.upper_ref, ...), custom_call_target="tpu_custom_call" | custom-call | flops 12683575296 | bytes 1048576 | tf_op jit(solution)/shard_map/weights/pallas_call | solution.py:373
  142.0 6.7 %all-to-all-start.1 = ((bf16[32,224,128]{2,1,0:T(8,128)(2,1)}), bf16[32,224,128]{2,1,0:T(8,128)(2,1)S(1)}, u32[]{:S(2)}, u32[]{:S(2)}) async-start(bf16[32,224,128]{2,1,0:T(8,128)(2,1)} %bitcast.26), calls=%async_computation.1 | async-start | bytes 3670016 | tf_op jit(solution)/shard_map/all_to_all | solution.py:391
  148.7 3.7 %collective-permute-start.4 = (bf16[256,128]{1,0:T(8,128)(2,1)S(1)}, bf16[256,128]{1,0:T(8,128)(2,1)S(1)}, u32[]{:S(2)}, u32[]{:S(2)}) collective-permute-start(bf16[256,128]{1,0:T(8,128)(2,1)S(1)} %copy-done.5), channel_id=1, source_target_pairs={{0,1},{1,2},{2,3},{3,4},{4,5},{5,6},{6,7},{7,8},{8,9},{9,10},{10,1... | collective-permute-start | bytes 196616 | tf_op jit(solution)/shard_map/ppermute | solution.py:25
  152.4 1.5 collective-permute-start.5
  153.9 44.2 %second_layer.1 = bf16[2048,128]{1,0:T(8,128)(2,1)} custom-call(s32[1]{0:T(128)} %copy.16.count_ref, s32[27,2048]{1,0:T(8,128)} %bitcast.35, s32[1,2048]{1,0:T(1,128)} %order_ref.3, bf16[2048,128]{1,0:T(8,128)(2,1)} %skip_ref.1, bf16[2048,128]{1,0:T(8,128)(2,1)} %get-tuple-element.33.field_ref, bf16[512,128]{1,0:T(8,128)(2,1)} %copy-done.2, ...), custom_call_target="tpu_custom_call" | custom-call | flops 50734301184 | bytes 1048576 | tf_op jit(solution)/shard_map/second_layer/pallas_call | solution.py:373
  199.2 1.6 pad_maximum_fusion
  200.8 6.7 %all-to-all-start.2 = ((bf16[32,288,128]{2,1,0:T(8,128)(2,1)}), bf16[32,288,128]{2,1,0:T(8,128)(2,1)S(1)}, u32[]{:S(2)}, u32[]{:S(2)}) async-start(bf16[32,288,128]{2,1,0:T(8,128)(2,1)} %pad_maximum_fusion), calls=%async_computation.2 | async-start | bytes 4718592 | tf_op jit(solution)/shard_map/all_to_all | solution.py:391
  208.2 0.6 copy-done.7
  208.8 39.0 %first_back.1 = bf16[2048,128]{1,0:T(8,128)(2,1)} custom-call(s32[1]{0:T(128)} %copy.16.count_ref, s32[27,2048]{1,0:T(8,128)} %bitcast.36, bf16[2048,128]{1,0:T(8,128)(2,1)} %get-tuple-element.38.grad_ref, bf16[2048,128]{1,0:T(8,128)(2,1)} %get-tuple-element.25.grad_ref.top_ref, bf16[256,128]{1,0:T(8,128)(2,1)} %copy-done.6, bf16[256,128]{1,0:T(8,128)(2,1)} %copy-done.7, ...), custom_call_target="tpu_custom_call" | custom-call | flops 50734301184 | bytes 1048576 | tf_op jit(solution)/shard_map/first_back/pallas_call | solution.py:373
  247.8 15.4 %all-to-all-done.2 = bf16[32,288,128]{2,1,0:T(8,128)(2,1)S(1)} async-done(((bf16[32,288,128]{2,1,0:T(8,128)(2,1)}), bf16[32,288,128]{2,1,0:T(8,128)(2,1)S(1)}, u32[]{:S(2)}, u32[]{:S(2)}) %all-to-all-start.2) | async-done | bytes 2359328 | tf_op jit(solution)/shard_map/all_to_all | solution.py:391
  263.9 2.2 fusion
  266.1 0.9 slice.42
  (32 shorter events, 3.6 us)
Async XLA Ops:
  2.4 17.3 %collective-permute-start.1 = (bf16[256,128]{1,0:T(8,128)(2,1)S(1)}, bf16[256,128]{1,0:T(8,128)(2,1)S(1)}, u32[]{:S(2)}, u32[]{:S(2)}) collective-permute-start(bf16[256,128]{1,0:T(8,128)(2,1)S(1)} %get-tuple-element.43), channel_id=1, source_target_pairs={{1,0},{2,1},{3,2},{4,3},{5,4},{6,5},{7,6},{8,7},{9,8},{10,9},{11,1... | collective-permute-start | bytes 196616 | tf_op jit(solution)/shard_map/ppermute | solution.py:25
  3.7 16.0 %collective-permute-start = (bf16[256,128]{1,0:T(8,128)(2,1)S(1)}, bf16[256,128]{1,0:T(8,128)(2,1)S(1)}, u32[]{:S(2)}, u32[]{:S(2)}) collective-permute-start(bf16[256,128]{1,0:T(8,128)(2,1)S(1)} %get-tuple-element.44), channel_id=1, source_target_pairs={{0,1},{1,2},{2,3},{3,4},{4,5},{5,6},{6,7},{7,8},{8,9},{9,10},{10,1... | collective-permute-start | bytes 196616 | tf_op jit(solution)/shard_map/ppermute | solution.py:25
  9.1 57.6 %all-to-all-start = ((bf16[32,64,128]{2,1,0:T(8,128)(2,1)}), bf16[32,64,128]{2,1,0:T(8,128)(2,1)S(1)}, u32[]{:S(2)}, u32[]{:S(2)}) async-start(bf16[32,64,128]{2,1,0:T(8,128)(2,1)} %bitcast.28), calls=%async_computation | async-start | bytes 1048576 | tf_op jit(solution)/shard_map/all_to_all | solution.py:391
  19.7 0.6 copy-start.8
  19.7 0.6 copy-start.9
  66.7 0.8 copy-start.1
  75.6 46.8 %collective-permute-start.2 = (bf16[512,128]{1,0:T(8,128)(2,1)}, bf16[512,128]{1,0:T(8,128)(2,1)S(1)}, u32[]{:S(2)}, u32[]{:S(2)}) collective-permute-start(bf16[512,128]{1,0:T(8,128)(2,1)} %get-tuple-element.27), channel_id=1, source_target_pairs={{0,1},{1,2},{2,3},{3,4},{4,5},{5,6},{6,7},{7,8},{8,9},{9,10},{10,1... | collective-permute-start | bytes 393224 | tf_op jit(solution)/shard_map/ppermute | solution.py:25
  79.3 43.1 %collective-permute-start.3 = (bf16[512,128]{1,0:T(8,128)(2,1)}, bf16[512,128]{1,0:T(8,128)(2,1)S(1)}, u32[]{:S(2)}, u32[]{:S(2)}) collective-permute-start(bf16[512,128]{1,0:T(8,128)(2,1)} %get-tuple-element.28), channel_id=1, source_target_pairs={{1,0},{2,1},{3,2},{4,3},{5,4},{6,5},{7,6},{8,7},{9,8},{10,9},{11,1... | collective-permute-start | bytes 393224 | tf_op jit(solution)/shard_map/ppermute | solution.py:25
  122.4 0.6 copy-start.2
  122.5 0.7 copy-start.3
  142.0 6.7 %copy-start.5 = (bf16[256,128]{1,0:T(8,128)(2,1)S(1)}, bf16[256,128]{1,0:T(8,128)(2,1)}, u32[]{:S(2)}) copy-start(bf16[256,128]{1,0:T(8,128)(2,1)} %get-tuple-element.39) | copy-start | bytes 196612
  142.0 10.4 %copy-start.4 = (bf16[256,128]{1,0:T(8,128)(2,1)S(1)}, bf16[256,128]{1,0:T(8,128)(2,1)}, u32[]{:S(2)}) copy-start(bf16[256,128]{1,0:T(8,128)(2,1)} %get-tuple-element.40) | copy-start | bytes 196612
  142.0 56.2 %all-to-all-start.1 = ((bf16[32,224,128]{2,1,0:T(8,128)(2,1)}), bf16[32,224,128]{2,1,0:T(8,128)(2,1)S(1)}, u32[]{:S(2)}, u32[]{:S(2)}) async-start(bf16[32,224,128]{2,1,0:T(8,128)(2,1)} %bitcast.26), calls=%async_computation.1 | async-start | bytes 3670016 | tf_op jit(solution)/shard_map/all_to_all | solution.py:391
  148.7 58.8 %collective-permute-start.4 = (bf16[256,128]{1,0:T(8,128)(2,1)S(1)}, bf16[256,128]{1,0:T(8,128)(2,1)S(1)}, u32[]{:S(2)}, u32[]{:S(2)}) collective-permute-start(bf16[256,128]{1,0:T(8,128)(2,1)S(1)} %copy-done.5), channel_id=1, source_target_pairs={{0,1},{1,2},{2,3},{3,4},{4,5},{5,6},{6,7},{7,8},{8,9},{9,10},{10,1... | collective-permute-start | bytes 196616 | tf_op jit(solution)/shard_map/ppermute | solution.py:25
  152.4 55.1 %collective-permute-start.5 = (bf16[256,128]{1,0:T(8,128)(2,1)S(1)}, bf16[256,128]{1,0:T(8,128)(2,1)S(1)}, u32[]{:S(2)}, u32[]{:S(2)}) collective-permute-start(bf16[256,128]{1,0:T(8,128)(2,1)S(1)} %copy-done.4), channel_id=1, source_target_pairs={{1,0},{2,1},{3,2},{4,3},{5,4},{6,5},{7,6},{8,7},{9,8},{10,9},{11,1... | collective-permute-start | bytes 196616 | tf_op jit(solution)/shard_map/ppermute | solution.py:25
  198.2 1.0 copy-start
  200.8 62.4 %all-to-all-start.2 = ((bf16[32,288,128]{2,1,0:T(8,128)(2,1)}), bf16[32,288,128]{2,1,0:T(8,128)(2,1)S(1)}, u32[]{:S(2)}, u32[]{:S(2)}) async-start(bf16[32,288,128]{2,1,0:T(8,128)(2,1)} %pad_maximum_fusion), calls=%async_computation.2 | async-start | bytes 4718592 | tf_op jit(solution)/shard_map/all_to_all | solution.py:391
  207.5 0.6 copy-start.6
  208.2 0.6 copy-start.7

commit v5 on v4

--- a/solution.py
+++ b/solution.py
@@ -94,17 +94,22 @@
     return unit, inv_std, normed, bent
 
 
+def map_row(map_ref, nth):
+    return pl.ds(nth + (nth >= map_ref.shape[0] // 2).astype(jnp.int32), 1)
+
+
 def gather_step(
-    map_ref, before_ref, after_ref, weight_ref, out_ref, table_ref, slots, chans, keep_ref=None
-):
-    step = pl.program_id(0)
-    unroll = weight_ref.shape[0]
-    weight = weight_ref[...].reshape(unroll * chans, chans)
+    map_ref, before_ref, after_ref, weight_refs, out_ref, table_ref, slots, chans, keep_ref=None
+):
+    step = pl.program_id(0)
+    unroll = len(weight_refs)
+    weight = jnp.concatenate([ref[0] for ref in weight_refs], axis=0)
     for start in range(0, slots, WIDE):
         size = min(WIDE, slots - start)
         found = []
         for u in range(unroll):
-            entry = lane_replicated(map_ref[pl.ds(step * unroll + u, 1), start : start + size])
+            row = map_ref[map_row(map_ref, step * unroll + u), start : start + size]
+            entry = lane_replicated(row)
             rows = pick(entry - F, table_ref, chans)
             parts = []
             for side, face_ref in enumerate((before_ref, after_ref)):
@@ -125,47 +130,53 @@
 
 
 def first_layer_body(
-    count_ref, map_ref, field_ref, before_ref, after_ref, weight_ref, gain_ref,
-    first_ref, hidden_ref, rows_ref, table_ref,
+    count_ref, map_ref, field_ref, before_ref, after_ref, gain_ref, weight_refs, centre_ref,
+    hidden_ref, unit_ref, inv_ref, slope_ref, rows_ref, first_ref, table_ref,
 ):
     slots, chans = field_ref.shape
     step = pl.program_id(0)
 
     @pl.when(step == 0)
     def _():
-        first_ref[...] = jnp.zeros_like(first_ref)
         for start in range(0, slots, B):
             field = field_ref[start : start + B, :].astype(jnp.float32)
             field = (field * alive(start, B, count_ref[0], chans)).astype(jnp.bfloat16)
             load_table(table_ref, field, start, B, chans)
+            first_ref[start : start + B, :] = mm(field, centre_ref[0])
 
     gather_step(
-        map_ref, before_ref, after_ref, weight_ref, first_ref, table_ref, slots, chans, rows_ref
+        map_ref, before_ref, after_ref, weight_refs, first_ref, table_ref, slots, chans, rows_ref
     )
 
     @pl.when(step == pl.num_programs(0) - 1)
     def _():
         for start in range(0, slots, B):
             at = slice(start, start + B)
-            _, _, normed, bent = normalise(first_ref[at, :], gain_ref[...])
+            unit, inv_std, normed, bent = normalise(first_ref[at, :], gain_ref[...])
             act = 0.5 * normed * (1.0 + bent)
-            hidden_ref[at, :] = (act * alive(start, B, count_ref[0], chans)).astype(jnp.bfloat16)
+            live = alive(start, B, count_ref[0], chans)
+            hidden_ref[at, :] = (act * live).astype(jnp.bfloat16)
+            inner = GELU_SCALE * (1.0 + 3.0 * GELU_CUBIC * (normed * normed))
+            slope = 0.5 * (1.0 + bent) + 0.5 * normed * (1.0 - bent * bent) * inner
+            unit_ref[at, :] = unit
+            inv_ref[at, :] = jnp.broadcast_to(inv_std, (B, chans))
+            slope_ref[at, :] = slope * live
 
 
 def second_layer_body(
-    count_ref, map_ref, order_ref, skip_ref, field_ref, below_ref, above_ref, weight_ref,
-    serial_ref, second_ref, table_ref,
+    count_ref, map_ref, order_ref, skip_ref, field_ref, below_ref, above_ref, weight_refs,
+    centre_ref, serial_ref, second_ref, table_ref,
 ):
     slots, chans = field_ref.shape
     step = pl.program_id(0)
 
     @pl.when(step == 0)
     def _():
-        second_ref[...] = jnp.zeros_like(second_ref)
+        second_ref[...] = mm(field_ref[...], centre_ref[0])
         load_table(table_ref, field_ref, 0, slots, chans)
 
     faces = (below_ref.at[pl.ds(F, F), :], above_ref.at[pl.ds(F, F), :])
-    gather_step(map_ref, *faces, weight_ref, second_ref, table_ref, slots, chans)
+    gather_step(map_ref, *faces, weight_refs, second_ref, table_ref, slots, chans)
 
     @pl.when(step == pl.num_programs(0) - 1)
     def _():
@@ -183,18 +194,18 @@
             )
 
 
-def edge_step(map_ref, weight_ref, grad_ref, edge_ref, near_ref=None):
+def edge_step(map_ref, weight_refs, grad_ref, edge_ref, near_ref=None):
     chans = grad_ref.shape[1]
     slots = grad_ref.shape[0]
     step = pl.program_id(0)
-    unroll = weight_ref.shape[0]
-    back = jnp.concatenate([weight_ref[u] for u in range(unroll)], axis=1)
+    unroll = len(weight_refs)
+    back = jnp.concatenate([ref[0] for ref in weight_refs], axis=1)
     for side in range(2):
         at = slice(side * F, (side + 1) * F)
         grad = grad_ref[at, :].astype(jnp.float32)
         sums = []
         for u in range(unroll):
-            row = map_ref[pl.ds(step * unroll + u, 1), at]
+            row = map_ref[map_row(map_ref, step * unroll + u), at]
             crossing = jnp.where(side_mask(lane_replicated(row), side, slots), grad, 0.0)
             sums.append(
                 mm(onehot_cols(row & (F - 1), F), crossing.astype(jnp.bfloat16)).astype(
@@ -208,17 +219,17 @@
         )
 
 
-def scatter_step(map_ref, weight_ref, grad_ref, total_ref, turned_ref=None, wgrad_ref=None):
+def scatter_step(map_ref, weight_refs, grad_ref, total_ref, turned_ref=None, wgrad_ref=None):
     slots, chans = grad_ref.shape
     groups = slots // B
     step = pl.program_id(0)
-    unroll = weight_ref.shape[0]
+    unroll = len(weight_refs)
     own = []
     for u in range(unroll):
-        row = map_ref[pl.ds(step * unroll + u, 1), :]
+        row = map_ref[map_row(map_ref, step * unroll + u), :]
         grad = grad_ref[...].astype(jnp.float32)
         own.append(drop(row - F, lane_replicated(row) - F, grad, groups).astype(jnp.bfloat16))
-    back = jnp.concatenate([weight_ref[u] for u in range(unroll)], axis=1)
+    back = jnp.concatenate([ref[0] for ref in weight_refs], axis=1)
     wide = None
     for a in range(groups):
         piece = jnp.concatenate(
@@ -235,7 +246,7 @@
 
 
 def second_edges_body(
-    count_ref, map_ref, order_ref, slotted_ref, ends_ref, weight_ref,
+    count_ref, map_ref, order_ref, slotted_ref, ends_ref, weight_refs, centre_ref,
     grad_ref, near_ref, up_ref, down_ref, edge_ref,
 ):
     slots, chans = slotted_ref.shape
@@ -254,7 +265,7 @@
                 placed[:, a * chans : (a + 1) * chans] * live
             ).astype(jnp.bfloat16)
 
-    edge_step(map_ref, weight_ref, grad_ref, edge_ref, near_ref)
+    edge_step(map_ref, weight_refs, grad_ref, edge_ref, near_ref)
 
     @pl.when(step == pl.num_programs(0) - 1)
     def _():
@@ -265,24 +276,28 @@
 
 
 def second_back_body(
-    count_ref, map_ref, grad_ref, field_ref, weight_ref, total_ref, wgrad_ref, turned_ref
+    count_ref, map_ref, grad_ref, field_ref, weight_refs, centre_ref,
+    total_ref, wgrad_ref, middle_ref, turned_ref,
 ):
     step = pl.program_id(0)
 
     @pl.when(step == 0)
     def _():
-        total_ref[...] = jnp.zeros_like(total_ref)
+        total_ref[...] = lax.dot_general(
+            grad_ref[...], centre_ref[0], NT, preferred_element_type=jnp.float32
+        )
         turned_ref[...] = field_ref[...].T
-
-    scatter_step(map_ref, weight_ref, grad_ref, total_ref, turned_ref, wgrad_ref)
+        middle_ref[...] = mm(turned_ref[...], grad_ref[...])
+
+    scatter_step(map_ref, weight_refs, grad_ref, total_ref, turned_ref, wgrad_ref)
 
 
 def weights_body(
-    count_ref, map_ref, first_ref, upper_ref, below_ref, above_ref, gain_ref,
-    weight_ref, rows_ref, near_ref, partial_ref,
+    count_ref, map_ref, unit_ref, inv_ref, slope_ref, upper_ref, below_ref, above_ref, gain_ref,
+    field_ref, middle_ref, weight_refs, centre_ref, rows_ref, near_ref, partial_ref,
     grad_ref, wgrad_ref, up_ref, down_ref, turned_ref, faces_ref, edge_ref,
 ):
-    slots, chans = first_ref.shape
+    slots, chans = unit_ref.shape
     step = pl.program_id(0)
     unroll = rows_ref.shape[0]
     half = wgrad_ref.shape[0] // 2
@@ -301,10 +316,8 @@
                 upper = upper + below_ref[:F, :].astype(jnp.float32)
             if start == F:
                 upper = upper + above_ref[:F, :].astype(jnp.float32)
-            unit, inv_std, normed, bent = normalise(first_ref[at, :], gain_ref[...])
-            inner = GELU_SCALE * (1.0 + 3.0 * GELU_CUBIC * (normed * normed))
-            slope = 0.5 * (1.0 + bent) + 0.5 * normed * (1.0 - bent * bent) * inner
-            grad_normed = slope * (upper * live)
+            unit, inv_std = unit_ref[at, :], inv_ref[at, :]
+            grad_normed = slope_ref[at, :] * upper
             gain_term = gain_term + jnp.sum(grad_normed * unit, axis=0, keepdims=True)
             grad_unit = grad_normed * gain_ref[...]
             centred = (
@@ -315,6 +328,12 @@
             grad = (inv_std * centred).astype(jnp.bfloat16)
             grad_ref[at, :] = grad
             turned_ref[:, at] = grad.T
+            field = (field_ref[at, :].astype(jnp.float32) * live).astype(jnp.bfloat16)
+            term = mm(turned_ref[:, at], field)
+            centre_term = term if start == 0 else centre_term + term
+        middle = (half - 1) // 2
+        wgrad_ref[middle] = centre_term.T.astype(jnp.bfloat16)
+        wgrad_ref[half + middle] = middle_ref[...].astype(jnp.bfloat16)
         row = lax.broadcasted_iota(jnp.int32, (chans, chans), 0)
         high = gain_term.astype(jnp.bfloat16).astype(jnp.float32)
         wgrad_ref[half - 1] = jnp.where(
@@ -322,13 +341,15 @@
         ).astype(jnp.bfloat16)
         wgrad_ref[2 * half - 1] = jnp.zeros((chans, chans), jnp.bfloat16)
 
-    edge_step(map_ref, weight_ref, grad_ref, edge_ref)
+    edge_step(map_ref, weight_refs, grad_ref, edge_ref)
     wide = mm(turned_ref[...], jnp.concatenate([rows_ref[u] for u in range(unroll)], axis=1))
     edge = mm(faces_ref[...], jnp.concatenate([near_ref[u] for u in range(unroll)], axis=1))
     for u in range(unroll):
         at = slice(u * chans, (u + 1) * chans)
-        wgrad_ref[step * unroll + u] = wide[:, at].T.astype(jnp.bfloat16)
-        wgrad_ref[half + step * unroll + u] = (partial_ref[u] + edge[:, at]).astype(jnp.bfloat16)
+        nth = step * unroll + u
+        nth = nth + (nth >= (half - 1) // 2).astype(jnp.int32)
+        wgrad_ref[nth] = wide[:, at].T.astype(jnp.bfloat16)
+        wgrad_ref[half + nth] = (partial_ref[u] + edge[:, at]).astype(jnp.bfloat16)
 
     @pl.when(step == pl.num_programs(0) - 1)
     def _():
@@ -337,19 +358,21 @@
 
 
 def first_back_body(
-    count_ref, map_ref, grad_ref, top_ref, from_prev_ref, from_next_ref, weight_ref,
-    out_ref, total_ref,
+    count_ref, map_ref, grad_ref, top_ref, from_prev_ref, from_next_ref, weight_refs,
+    centre_ref, out_ref, total_ref,
 ):
     slots, chans = grad_ref.shape
     step = pl.program_id(0)
 
     @pl.when(step == 0)
     def _():
-        total_ref[...] = top_ref[...].astype(jnp.float32)
+        total_ref[...] = top_ref[...].astype(jnp.float32) + lax.dot_general(
+            grad_ref[...], centre_ref[0], NT, preferred_element_type=jnp.float32
+        )
         total_ref[:F, :] += from_prev_ref[...].astype(jnp.float32)
         total_ref[F : 2 * F, :] += from_next_ref[...].astype(jnp.float32)
 
-    scatter_step(map_ref, weight_ref, grad_ref, total_ref)
+    scatter_step(map_ref, weight_refs, grad_ref, total_ref)
 
     @pl.when(step == pl.num_programs(0) - 1)
     def _():
@@ -357,24 +380,43 @@
         out_ref[...] = (total_ref[...] * live).astype(jnp.bfloat16)
 
 
-def call(body, name, operands, stepped, outputs, scratch, together=3, dense=True):
-    offsets = operands[stepped[0]].shape[0]
-    unroll = together if offsets % together == 0 else 1
-    slots, chans = operands[1].shape[1], operands[stepped[0]].shape[2]
+def call(body, name, operands, weights, stepped, outputs, scratch, together=2, dense=True):
+    offsets, slots = operands[1].shape
+    chans = weights.shape[2]
+    centre = offsets // 2
+    count = offsets - 1
+    unroll = together if count % together == 0 else 1
     width = slots if dense else 4 * chans
 
-    def spec(shape, cut):
-        if cut:
-            return pl.BlockSpec((unroll,) + shape[1:], lambda k: (k,) + (0,) * (len(shape) - 1))
+    def whole(shape):
         return pl.BlockSpec(shape, lambda k: (0,) * len(shape))
 
+    def cut(shape):
+        return pl.BlockSpec((unroll,) + shape[1:], lambda k: (k,) + (0,) * (len(shape) - 1))
+
+    def nth_weight(u):
+        def at(k):
+            nth = k * unroll + u
+            return (jnp.where(nth >= centre, nth + 1, nth), 0, 0)
+
+        return pl.BlockSpec((1, chans, chans), at)
+
+    split = len(operands)
+
+    def wrapped(*refs):
+        after = split + unroll
+        body(*refs[:split], refs[split:after], *refs[after:])
+
     specs = [pl.BlockSpec(memory_space=pltpu.SMEM)]
-    specs += [spec(o.shape, n in stepped) for n, o in enumerate(operands) if n > 0]
+    specs += [whole(operand.shape) for operand in operands[1:]]
+    specs += [nth_weight(u) for u in range(unroll)]
+    specs.append(pl.BlockSpec((1, chans, chans), lambda k: (centre, 0, 0)))
+    specs += [cut(operand.shape) for operand in stepped]
     return pl.pallas_call(
-        body,
-        grid=(offsets // unroll,),
+        wrapped,
+        grid=(count // unroll,),
         in_specs=specs,
-        out_specs=[spec(out[0], len(out) > 2) for out in outputs],
+        out_specs=[cut(out[0]) if len(out) > 2 else whole(out[0]) for out in outputs],
         out_shape=[jax.ShapeDtypeStruct(out[0], out[1]) for out in outputs],
         scratch_shapes=[pltpu.VMEM(shape, dtype) for shape, dtype in scratch],
         compiler_params=PARAMS,
@@ -384,7 +426,7 @@
             bytes_accessed=4 * slots * chans,
         ),
         name=name,
-    )(*operands)
+    )(*operands, *([weights] * (unroll + 1)), *stepped)
 
 
 def swap_rows(rows):
@@ -409,38 +451,39 @@
     ends_x = (features[: 2 * F].astype(f32) * ends.astype(f32)).astype(bf16)
     before_x, after_x = shifted(ends_x[F:], 1), shifted(ends_x[:F], -1)
     slotted = swap_rows(cotangent)
-    first, hidden, rows_x = call(
+    hidden, unit, inv_std, slope, rows_x = call(
         first_layer_body, "first_layer",
-        (counts, neighbours, features, before_x, after_x, first_weight, gain), (5,),
-        (rows32, rows16, ((offsets, slots, chans), bf16, True)), (table16,),
+        (counts, neighbours, features, before_x, after_x, gain), first_weight, (),
+        (rows16, rows32, rows32, rows32, ((offsets - 1, slots, chans), bf16, True)),
+        (rows32, table16),
     )
     edge32 = ((2 * F, chans), f32)
     ends16 = ((2 * F, chans), bf16)
     grad_live, near, upper_up, upper_down = call(
         second_edges_body, "second_edges",
-        (counts, neighbours, send_order, slotted, hidden[: 2 * F], second_weight), (5,),
-        (rows16, ((offsets, 2 * F, chans), bf16, True), ends16, ends16), (edge32,), 9, False,
+        (counts, neighbours, send_order, slotted, hidden[: 2 * F]), second_weight, (),
+        (rows16, ((offsets - 1, 2 * F, chans), bf16, True), ends16, ends16), (edge32,), 13, False,
     )
     below, above = shifted(upper_up, 1), shifted(upper_down, -1)
-    upper, partial = call(
+    upper, partial, middle = call(
         second_back_body, "second_back",
-        (counts, neighbours, grad_live, hidden, second_weight), (4,),
-        (rows32, ((offsets, chans, chans), f32, True)), (turned16,),
+        (counts, neighbours, grad_live, hidden), second_weight, (),
+        (rows32, ((offsets - 1, chans, chans), f32, True), ((chans, chans), f32)), (turned16,),
     )
     grad_first, wgrads, lower_up, lower_down = call(
         weights_body, "weights",
-        (counts, neighbours, first, upper, below, above, gain, first_weight, rows_x, near,
-         partial), (7, 8, 9, 10),
+        (counts, neighbours, unit, inv_std, slope, upper, below, above, gain, features, middle),
+        first_weight, (rows_x, near, partial),
         (rows16, ((2 * (offsets + 1), chans, chans), bf16), face16, face16),
-        (turned16, ((chans, 2 * F), bf16), edge32), 3, False,
+        (turned16, ((chans, 2 * F), bf16), edge32), 2, False,
     )
     from_prev, from_next = shifted(lower_up, 1), shifted(lower_down, -1)
     parts = swap_rows(wgrads.reshape(devices, -1, chans))
     hidden, grad_first = lax.optimization_barrier((hidden, grad_first))
     (ordered,) = call(
         second_layer_body, "second_layer",
-        (counts, neighbours, send_order, features, hidden, below, above, second_weight),
-        (7,), (rows16,), (rows32, table16),
+        (counts, neighbours, send_order, features, hidden, below, above), second_weight,
+        (), (rows16,), (rows32, table16),
     )
     part = jnp.sum(parts.astype(f32), axis=0).astype(bf16)
     ordered, part, grad_first = lax.optimization_barrier((ordered, part, grad_first))
@@ -458,7 +501,7 @@
     shared = both[:, per_peer:]
     (grad_features,) = call(
         first_back_body, "first_back",
-        (counts, neighbours, grad_first, grad_live, from_prev, from_next, first_weight), (6,),
+        (counts, neighbours, grad_first, grad_live, from_prev, from_next), first_weight, (),
         (rows16,), (rows32,),
     )
     shared = shared.reshape(2, offsets + 1, chans, chans)

time: 268 us -> 273 us (1.019)
  Pallas kernels: 197 us -> 202 us
    pallas_call x6, Pallas kernels: 197 us -> 202 us  [call(): pl.pallas_call(wrapped, grid=(count // unroll,), in_specs=specs, out_spec...]
where the time goes in v5:
time: 273 us; the launch traced here: 272 us
  Pallas kernels  202 us (74%)
  starting transfers between devices  39.3 us (14%)
  waiting for transfers between devices  15 us (5%)
  local copies, waits for them, and re-layouts  8.4 us (3%)
  other arithmetic  5.61 us (2%)
    pallas_call x6, Pallas kernels, call(): pl.pallas_call(wrapped, grid=(count // unroll,), in_specs=specs, out_spec...  202 us
    all_to_all x3, starting transfers between devices, swap_rows(): return lax.all_to_all(rows, AXES, split_axis=0, concat_axis=0, tiled=True)  22.4 us
    ppermute x6, starting transfers between devices, shifted(): lax.ppermute(value, AXES, [(source, source + steps) for source in range(i...  16.9 us
    all_to_all x3, waiting for transfers between devices, swap_rows(): return lax.all_to_all(rows, AXES, split_axis=0, concat_axis=0, tiled=True)  14.9 us
    unnamed x21, local copies, waits for them, and re-layouts  5.6 us
  transfers between devices with their start and end apart: 9, of which 1 were waited for; matrix products, arithmetic and copies ran while one was open for 2% of the time, Pallas kernels for 64%

profile of v5, /device:TPU:0, one launch (start us, length us, event | category | flops | bytes accessed | tf_op | source)
XLA Modules:
  0.0 271.7 jit_solution(1693904542487483745)
XLA Ops:
  1.3 1.0 multiply_convert_fusion
  2.4 1.3 collective-permute-start.1
  3.7 5.5 %collective-permute-start = (bf16[256,128]{1,0:T(8,128)(2,1)S(1)}, bf16[256,128]{1,0:T(8,128)(2,1)S(1)}, u32[]{:S(2)}, u32[]{:S(2)}) collective-permute-start(bf16[256,128]{1,0:T(8,128)(2,1)S(1)} %get-tuple-element.50), channel_id=1, source_target_pairs={{0,1},{1,2},{2,3},{3,4},{4,5},{5,6},{6,7},{7,8},{8,9},{9,10},{10,1... | collective-permute-start | bytes 196616 | tf_op jit(solution)/shard_map/ppermute | solution.py:25
  9.1 8.8 %all-to-all-start = ((bf16[32,64,128]{2,1,0:T(8,128)(2,1)}), bf16[32,64,128]{2,1,0:T(8,128)(2,1)S(1)}, u32[]{:S(2)}, u32[]{:S(2)}) async-start(bf16[32,64,128]{2,1,0:T(8,128)(2,1)} %bitcast.28), calls=%async_computation | async-start | bytes 1048576 | tf_op jit(solution)/shard_map/all_to_all | solution.py:433
  17.9 1.7 copy.15
  20.3 47.8 %first_layer.1 = (bf16[2048,128]{1,0:T(8,128)(2,1)}, f32[2048,128]{1,0:T(8,128)}, f32[2048,128]{1,0:T(8,128)}, f32[2048,128]{1,0:T(8,128)}, bf16[26,2048,128]{2,1,0:T(8,128)(2,1)}) custom-call(s32[1]{0:T(128)} %copy.16.refs_0_, s32[27,2048]{1,0:T(8,128)} %bitcast.31, bf16[2048,128]{1,0:T(8,128)(2,1)} %refs_3_.1, bf16[256,128]{1,0:T(8,128)(2,1)} %copy-done.9, ...), custom_call_target="tpu_custom_call" | custom-call | flops 50734301184 | bytes 1048576 | tf_op jit(solution)/shard_map/first_layer/pallas_call | solution.py:415
  68.1 1.6 slice.33.refs_4_
  69.7 0.8 copy-done.1
  70.5 8.4 %second_edges.1 = (bf16[2048,128]{1,0:T(8,128)(2,1)}, bf16[26,512,128]{2,1,0:T(8,128)(2,1)}, bf16[512,128]{1,0:T(8,128)(2,1)}, bf16[512,128]{1,0:T(8,128)(2,1)}) custom-call(s32[1]{0:T(128)} %copy.16.refs_0_, s32[27,2048]{1,0:T(8,128)} %bitcast.32, s32[1,2048]{1,0:T(1,128)} %refs_2_.5, bf16[2048,128]{1,0:T(8,128)(2,1)} %bitcast.29, ...), custom_call_target="tpu_custom_call" | custom-call | flops 12683575296 | bytes 1048576 | tf_op jit(solution)/shard_map/second_edges/pallas_call | solution.py:415
  78.9 3.7 %collective-permute-start.2 = (bf16[512,128]{1,0:T(8,128)(2,1)}, bf16[512,128]{1,0:T(8,128)(2,1)S(1)}, u32[]{:S(2)}, u32[]{:S(2)}) collective-permute-start(bf16[512,128]{1,0:T(8,128)(2,1)} %get-tuple-element.32), channel_id=1, source_target_pairs={{0,1},{1,2},{2,3},{3,4},{4,5},{5,6},{6,7},{7,8},{8,9},{9,10},{10,1... | collective-permute-start | bytes 393224 | tf_op jit(solution)/shard_map/ppermute | solution.py:25
  82.6 1.5 collective-permute-start.3
  84.1 41.2 %second_back.1 = (f32[2048,128]{1,0:T(8,128)}, f32[26,128,128]{2,1,0:T(8,128)}, f32[128,128]{1,0:T(8,128)}) custom-call(s32[1]{0:T(128)} %copy.16.refs_0_, s32[27,2048]{1,0:T(8,128)} %bitcast.33, bf16[2048,128]{1,0:T(8,128)(2,1)} %get-tuple-element.30.refs_2_.refs_3_, bf16[2048,128]{1,0:T(8,128)(2,1)} %get-tuple-element.39.refs_3_.refs_4_, ...), custom_call_target="tpu_custom_call" | custom-call | flops 50734301184 | bytes 1048576 | tf_op jit(solution)/shard_map/second_back/pallas_call | solution.py:415
  125.3 0.6 copy-done.2
  126.0 19.4 %weights.1 = (bf16[2048,128]{1,0:T(8,128)(2,1)}, bf16[56,128,128]{2,1,0:T(8,128)(2,1)}, bf16[256,128]{1,0:T(8,128)(2,1)}, bf16[256,128]{1,0:T(8,128)(2,1)}) custom-call(s32[1]{0:T(128)} %copy.16.refs_0_, s32[27,2048]{1,0:T(8,128)} %bitcast.34, f32[2048,128]{1,0:T(8,128)} %get-tuple-element.27.refs_2_, f32[2048,128]{1,0:T(8,128)} %get-tuple-element.28.refs_3_, ...), custom_call_target="tpu_custom_call" | custom-call | flops 12683575296 | bytes 1048576 | tf_op jit(solution)/shard_map/weights/pallas_call | solution.py:415
  145.4 6.7 %all-to-all-start.1 = ((bf16[32,224,128]{2,1,0:T(8,128)(2,1)}), bf16[32,224,128]{2,1,0:T(8,128)(2,1)S(1)}, u32[]{:S(2)}, u32[]{:S(2)}) async-start(bf16[32,224,128]{2,1,0:T(8,128)(2,1)} %bitcast.26), calls=%async_computation.1 | async-start | bytes 3670016 | tf_op jit(solution)/shard_map/all_to_all | solution.py:433
  152.2 3.7 %collective-permute-start.4 = (bf16[256,128]{1,0:T(8,128)(2,1)S(1)}, bf16[256,128]{1,0:T(8,128)(2,1)S(1)}, u32[]{:S(2)}, u32[]{:S(2)}) collective-permute-start(bf16[256,128]{1,0:T(8,128)(2,1)S(1)} %copy-done.5), channel_id=1, source_target_pairs={{0,1},{1,2},{2,3},{3,4},{4,5},{5,6},{6,7},{7,8},{8,9},{9,10},{10,1... | collective-permute-start | bytes 196616 | tf_op jit(solution)/shard_map/ppermute | solution.py:25
  155.8 1.3 collective-permute-start.5
  157.1 45.7 %second_layer.1 = bf16[2048,128]{1,0:T(8,128)(2,1)} custom-call(s32[1]{0:T(128)} %copy.16.refs_0_, s32[27,2048]{1,0:T(8,128)} %bitcast.35, s32[1,2048]{1,0:T(1,128)} %refs_2_.5, bf16[2048,128]{1,0:T(8,128)(2,1)} %refs_3_.1, bf16[2048,128]{1,0:T(8,128)(2,1)} %get-tuple-element.39.refs_3_.refs_4_, bf16[512,128]{1,0:T(8,128)(2,1)} %copy-done.2, ...), custom_call_target="tpu_custom_call" | custom-call | flops 50734301184 | bytes 1048576 | tf_op jit(solution)/shard_map/second_layer/pallas_call | solution.py:415
  203.9 1.6 pad_maximum_fusion
  205.5 6.9 %all-to-all-start.2 = ((bf16[32,288,128]{2,1,0:T(8,128)(2,1)}), bf16[32,288,128]{2,1,0:T(8,128)(2,1)S(1)}, u32[]{:S(2)}, u32[]{:S(2)}) async-start(bf16[32,288,128]{2,1,0:T(8,128)(2,1)} %pad_maximum_fusion), calls=%async_computation.2 | async-start | bytes 4718592 | tf_op jit(solution)/shard_map/all_to_all | solution.py:433
  213.7 39.3 %first_back.1 = bf16[2048,128]{1,0:T(8,128)(2,1)} custom-call(s32[1]{0:T(128)} %copy.16.refs_0_, s32[27,2048]{1,0:T(8,128)} %bitcast.36, bf16[2048,128]{1,0:T(8,128)(2,1)} %get-tuple-element.44.refs_2_, bf16[2048,128]{1,0:T(8,128)(2,1)} %get-tuple-element.30.refs_2_.refs_3_, bf16[256,128]{1,0:T(8,128)(2,1)} %copy-done.6, bf16[256,128]{1,0:T(8,128)(2,1)} %copy-done.7, ...), custom_call_target="tpu_custom_call" | custom-call | flops 50734301184 | bytes 1048576 | tf_op jit(solution)/shard_map/first_back/pallas_call | solution.py:415
  253.0 14.9 %all-to-all-done.2 = bf16[32,288,128]{2,1,0:T(8,128)(2,1)S(1)} async-done(((bf16[32,288,128]{2,1,0:T(8,128)(2,1)}), bf16[32,288,128]{2,1,0:T(8,128)(2,1)S(1)}, u32[]{:S(2)}, u32[]{:S(2)}) %all-to-all-start.2) | async-done | bytes 2359328 | tf_op jit(solution)/shard_map/all_to_all | solution.py:433
  268.6 2.2 fusion
  270.8 0.9 slice.42
  (32 shorter events, 3.6 us)
Async XLA Ops:
  2.4 17.3 %collective-permute-start.1 = (bf16[256,128]{1,0:T(8,128)(2,1)S(1)}, bf16[256,128]{1,0:T(8,128)(2,1)S(1)}, u32[]{:S(2)}, u32[]{:S(2)}) collective-permute-start(bf16[256,128]{1,0:T(8,128)(2,1)S(1)} %get-tuple-element.49), channel_id=1, source_target_pairs={{1,0},{2,1},{3,2},{4,3},{5,4},{6,5},{7,6},{8,7},{9,8},{10,9},{11,1... | collective-permute-start | bytes 196616 | tf_op jit(solution)/shard_map/ppermute | solution.py:25
  3.7 16.0 %collective-permute-start = (bf16[256,128]{1,0:T(8,128)(2,1)S(1)}, bf16[256,128]{1,0:T(8,128)(2,1)S(1)}, u32[]{:S(2)}, u32[]{:S(2)}) collective-permute-start(bf16[256,128]{1,0:T(8,128)(2,1)S(1)} %get-tuple-element.50), channel_id=1, source_target_pairs={{0,1},{1,2},{2,3},{3,4},{4,5},{5,6},{6,7},{7,8},{8,9},{9,10},{10,1... | collective-permute-start | bytes 196616 | tf_op jit(solution)/shard_map/ppermute | solution.py:25
  9.1 60.6 %all-to-all-start = ((bf16[32,64,128]{2,1,0:T(8,128)(2,1)}), bf16[32,64,128]{2,1,0:T(8,128)(2,1)S(1)}, u32[]{:S(2)}, u32[]{:S(2)}) async-start(bf16[32,64,128]{2,1,0:T(8,128)(2,1)} %bitcast.28), calls=%async_computation | async-start | bytes 1048576 | tf_op jit(solution)/shard_map/all_to_all | solution.py:433
  19.7 0.6 copy-start.8
  19.7 0.6 copy-start.9
  69.7 0.8 copy-start.1
  78.9 46.4 %collective-permute-start.2 = (bf16[512,128]{1,0:T(8,128)(2,1)}, bf16[512,128]{1,0:T(8,128)(2,1)S(1)}, u32[]{:S(2)}, u32[]{:S(2)}) collective-permute-start(bf16[512,128]{1,0:T(8,128)(2,1)} %get-tuple-element.32), channel_id=1, source_target_pairs={{0,1},{1,2},{2,3},{3,4},{4,5},{5,6},{6,7},{7,8},{8,9},{9,10},{10,1... | collective-permute-start | bytes 393224 | tf_op jit(solution)/shard_map/ppermute | solution.py:25
  82.6 42.7 %collective-permute-start.3 = (bf16[512,128]{1,0:T(8,128)(2,1)}, bf16[512,128]{1,0:T(8,128)(2,1)S(1)}, u32[]{:S(2)}, u32[]{:S(2)}) collective-permute-start(bf16[512,128]{1,0:T(8,128)(2,1)} %get-tuple-element.33), channel_id=1, source_target_pairs={{1,0},{2,1},{3,2},{4,3},{5,4},{6,5},{7,6},{8,7},{9,8},{10,9},{11,1... | collective-permute-start | bytes 393224 | tf_op jit(solution)/shard_map/ppermute | solution.py:25
  125.3 0.7 copy-start.2
  125.3 0.7 copy-start.3
  145.4 6.7 %copy-start.5 = (bf16[256,128]{1,0:T(8,128)(2,1)S(1)}, bf16[256,128]{1,0:T(8,128)(2,1)}, u32[]{:S(2)}) copy-start(bf16[256,128]{1,0:T(8,128)(2,1)} %get-tuple-element.45) | copy-start | bytes 196612
  145.4 10.4 %copy-start.4 = (bf16[256,128]{1,0:T(8,128)(2,1)S(1)}, bf16[256,128]{1,0:T(8,128)(2,1)}, u32[]{:S(2)}) copy-start(bf16[256,128]{1,0:T(8,128)(2,1)} %get-tuple-element.46) | copy-start | bytes 196612
  145.4 57.5 %all-to-all-start.1 = ((bf16[32,224,128]{2,1,0:T(8,128)(2,1)}), bf16[32,224,128]{2,1,0:T(8,128)(2,1)S(1)}, u32[]{:S(2)}, u32[]{:S(2)}) async-start(bf16[32,224,128]{2,1,0:T(8,128)(2,1)} %bitcast.26), calls=%async_computation.1 | async-start | bytes 3670016 | tf_op jit(solution)/shard_map/all_to_all | solution.py:433
  152.2 60.3 %collective-permute-start.4 = (bf16[256,128]{1,0:T(8,128)(2,1)S(1)}, bf16[256,128]{1,0:T(8,128)(2,1)S(1)}, u32[]{:S(2)}, u32[]{:S(2)}) collective-permute-start(bf16[256,128]{1,0:T(8,128)(2,1)S(1)} %copy-done.5), channel_id=1, source_target_pairs={{0,1},{1,2},{2,3},{3,4},{4,5},{5,6},{6,7},{7,8},{8,9},{9,10},{10,1... | collective-permute-start | bytes 196616 | tf_op jit(solution)/shard_map/ppermute | solution.py:25
  155.8 56.6 %collective-permute-start.5 = (bf16[256,128]{1,0:T(8,128)(2,1)S(1)}, bf16[256,128]{1,0:T(8,128)(2,1)S(1)}, u32[]{:S(2)}, u32[]{:S(2)}) collective-permute-start(bf16[256,128]{1,0:T(8,128)(2,1)S(1)} %copy-done.4), channel_id=1, source_target_pairs={{1,0},{2,1},{3,2},{4,3},{5,4},{6,5},{7,6},{8,7},{9,8},{10,9},{11,1... | collective-permute-start | bytes 196616 | tf_op jit(solution)/shard_map/ppermute | solution.py:25
  202.9 1.0 copy-start
  205.5 62.4 %all-to-all-start.2 = ((bf16[32,288,128]{2,1,0:T(8,128)(2,1)}), bf16[32,288,128]{2,1,0:T(8,128)(2,1)S(1)}, u32[]{:S(2)}, u32[]{:S(2)}) async-start(bf16[32,288,128]{2,1,0:T(8,128)(2,1)} %pad_maximum_fusion), calls=%async_computation.2 | async-start | bytes 4718592 | tf_op jit(solution)/shard_map/all_to_all | solution.py:433
  212.4 0.6 copy-start.6
  213.1 0.6 copy-start.7
